TPU v7x, 32 devices: a whole 2x2x4 slice. The times are simulated.
32 devices in a mesh: fsdp: 8 (over y, x, core), tp: 4 (over z).
Axes of the slice: x: 2, y: 2, z: 4, core: 2. Of those that a mesh axis runs over, the one named last changes fastest.
Arguments:
- inputs: bfloat16 [2, 16384, 1024], P(None, ('fsdp', 'tp')), may hold values from -6 to 6
- w_query: bfloat16 [1024, 1024], P('fsdp', 'tp'), may hold values from -0.1875 to 0.1875
- w_key: bfloat16 [1024, 1024], P('fsdp', 'tp'), may hold values from -0.375 to 0.375
- w_value: bfloat16 [1024, 1024], P('fsdp', 'tp'), may hold values from -0.1875 to 0.1875
- b_query: bfloat16 [4, 256], P('tp', 'fsdp'), may hold values from -3 to 3
- b_value: bfloat16 [4, 256], P('tp', 'fsdp'), may hold values from -0.59765625 to 0.59765625
- w_output: bfloat16 [1024, 1024], P('tp', 'fsdp'), may hold values from -0.75 to 0.75
- b_output: bfloat16 [1024], P(('fsdp', 'tp')), may hold values from -1.796875 to 1.796875
- attn_gain: bfloat16 [1024], P(('fsdp', 'tp')), may hold values from 0.25 to 1.75
- attn_shift: bfloat16 [1024], P(('fsdp', 'tp')), may hold values from -1.796875 to 1.796875
- w_up: bfloat16 [1024, 4096], P('fsdp', 'tp'), may hold values from -0.1875 to 0.1875
- b_up: bfloat16 [4, 1024], P('tp', 'fsdp'), may hold values from -3 to 3
- w_down: bfloat16 [4096, 1024], P('tp', 'fsdp'), may hold values from -0.09375 to 0.09375
- b_down: bfloat16 [1024], P(('fsdp', 'tp')), may hold values from -1.796875 to 1.796875
- mlp_gain: bfloat16 [1024], P(('fsdp', 'tp')), may hold values from 0.25 to 1.75
- mlp_shift: bfloat16 [1024], P(('fsdp', 'tp')), may hold values from -1.796875 to 1.796875
- doc_lengths: int32 [2, 8, 8], P(None, 'fsdp'), may hold values from 1 to 1536, 2048 in all within a row
- out_grad: bfloat16 [2, 16384, 1024], P(None, ('fsdp', 'tp')), may hold values from -6 to 6
Outputs:
- layer_out: bfloat16 [2, 16384, 1024], P(None, ('fsdp', 'tp'))
- input_grad: bfloat16 [2, 16384, 1024], P(None, ('fsdp', 'tp'))
- grad_w_query: float32 [1024, 1024], P('fsdp', 'tp')
- grad_w_key: float32 [1024, 1024], P('fsdp', 'tp')
- grad_w_value: float32 [1024, 1024], P('fsdp', 'tp')
- grad_b_query: float32 [4, 256], P('tp', 'fsdp')
- grad_b_value: float32 [4, 256], P('tp', 'fsdp')
- grad_w_output: float32 [1024, 1024], P('tp', 'fsdp')
- grad_b_output: float32 [1024], P(('fsdp', 'tp'))
- grad_attn_gain: float32 [1024], P(('fsdp', 'tp'))
- grad_attn_shift: float32 [1024], P(('fsdp', 'tp'))
- grad_w_up: float32 [1024, 4096], P('fsdp', 'tp')
- grad_b_up: float32 [4, 1024], P('tp', 'fsdp')
- grad_w_down: float32 [4096, 1024], P('tp', 'fsdp')
- grad_b_down: float32 [1024], P(('fsdp', 'tp'))
- grad_mlp_gain: float32 [1024], P(('fsdp', 'tp'))
- grad_mlp_shift: float32 [1024], P(('fsdp', 'tp'))
Inputs may be any that keep to these rules, and one draw needn't show every extreme that they name: `doc_lengths`: each sequence's 8 lengths sum to 2048, and its longest document has exactly 1536 tokens.
All inputs are finite; a program needn't handle non-finite values.
Results may differ from a plain program's by a relative error of at most 0.02.
Values may be sent and summed in bfloat16 or wider, within the bound.
No kernel may reach another device: no remote copies, remote signals or barrier semaphores. Data moves between devices by JAX's collectives and lax.ppermute only.
A program may use at most 512 MiB of HBM per device.

v0:
```python
from functools import partial

import jax
import jax.numpy as jnp
from jax import lax
from jax.sharding import PartitionSpec as P

HEAD_DIM = 64
WINDOW = 1024


EPSILON = 1e-12
MASKED = -1000000000.0


def norm_forward(values, norm_gain, norm_bias):
    average = jnp.mean(values, axis=-1, keepdims=True)
    centred = values - average
    inverse = lax.rsqrt(jnp.mean(centred * centred, axis=-1, keepdims=True) + EPSILON)
    normed = centred * inverse
    return (normed * norm_gain + norm_bias, normed, inverse)


def norm_backward(upstream, normed, inverse, norm_gain):
    scaled = upstream * norm_gain
    inner_mean = jnp.mean(scaled, axis=-1, keepdims=True)
    cross_mean = jnp.mean(scaled * normed, axis=-1, keepdims=True)
    values_grad = inverse * (scaled - inner_mean - normed * cross_mean)
    return (values_grad, jnp.sum(upstream * normed, axis=0), jnp.sum(upstream, axis=0))


def segment_ids(lengths, seq_len):
    doc_ends = jnp.cumsum(lengths)
    places = jnp.arange(seq_len, dtype=jnp.int32)
    segments = jnp.sum((places[:, None] >= doc_ends[None, :]).astype(jnp.int32), axis=1)
    return (segments, places)


def block_scores(query_heads, key_heads, segments, places, row_start, block_rows):
    seg_rows = segments[row_start : row_start + block_rows]
    place_rows = places[row_start : row_start + block_rows]
    allowed = (seg_rows[:, None] == segments[None, :]) & (
        jnp.abs(place_rows[:, None] - places[None, :]) < WINDOW
    )
    scores = jnp.einsum(
        "qhd,khd->hqk", query_heads, key_heads, preferred_element_type=jnp.float32
    ) * HEAD_DIM ** (-0.5)
    return jnp.where(allowed[None], scores, MASKED)


def attention_forward(query_rows, key_rows, value_rows, segments, places):
    seq_len, col_count = query_rows.shape
    head_count = col_count // HEAD_DIM
    block_rows = min(512, seq_len)
    key_heads = key_rows.reshape(seq_len, head_count, HEAD_DIM)
    value_heads = value_rows.reshape(seq_len, head_count, HEAD_DIM)
    outputs = []
    logsums = []
    for row_start in range(0, seq_len, block_rows):
        query_heads = query_rows[row_start : row_start + block_rows].reshape(
            block_rows, head_count, HEAD_DIM
        )
        scores = block_scores(query_heads, key_heads, segments, places, row_start, block_rows)
        row_top = jnp.max(scores, axis=-1, keepdims=True)
        exponent = jnp.exp(scores - row_top)
        row_total = jnp.sum(exponent, axis=-1, keepdims=True)
        attn_probs = (exponent / row_total).astype(jnp.bfloat16)
        context = jnp.einsum(
            "hqk,khd->qhd", attn_probs, value_heads, preferred_element_type=jnp.float32
        )
        outputs.append(context.reshape(block_rows, col_count))
        logsums.append(row_top + jnp.log(row_total))
    return (jnp.concatenate(outputs, axis=0).astype(jnp.bfloat16), jnp.concatenate(logsums, axis=1))


def attention_backward(query_rows, key_rows, value_rows, context_grad, logsums, segments, places):
    seq_len, col_count = query_rows.shape
    head_count = col_count // HEAD_DIM
    score_scale = HEAD_DIM ** (-0.5)
    block_rows = min(512, seq_len)
    key_heads = key_rows.reshape(seq_len, head_count, HEAD_DIM)
    value_heads = value_rows.reshape(seq_len, head_count, HEAD_DIM)
    key_grad = jnp.zeros((seq_len, head_count, HEAD_DIM), jnp.float32)
    value_grad = jnp.zeros((seq_len, head_count, HEAD_DIM), jnp.float32)
    query_parts = []
    for row_start in range(0, seq_len, block_rows):
        query_heads = query_rows[row_start : row_start + block_rows].reshape(
            block_rows, head_count, HEAD_DIM
        )
        grad_heads = context_grad[row_start : row_start + block_rows].reshape(
            block_rows, head_count, HEAD_DIM
        )
        scores = block_scores(query_heads, key_heads, segments, places, row_start, block_rows)
        attn_probs = jnp.exp(scores - logsums[:, row_start : row_start + block_rows])
        value_grad = value_grad + jnp.einsum(
            "hqk,qhd->khd",
            attn_probs.astype(jnp.bfloat16),
            grad_heads,
            preferred_element_type=jnp.float32,
        )
        prob_grad = jnp.einsum(
            "qhd,khd->hqk", grad_heads, value_heads, preferred_element_type=jnp.float32
        )
        row_delta = jnp.sum(attn_probs * prob_grad, axis=-1, keepdims=True)
        score_grad = (attn_probs * (prob_grad - row_delta)).astype(jnp.bfloat16)
        query_part = (
            jnp.einsum("hqk,khd->qhd", score_grad, key_heads, preferred_element_type=jnp.float32)
            * score_scale
        )
        query_parts.append(query_part.astype(jnp.bfloat16).reshape(block_rows, col_count))
        key_grad = (
            key_grad
            + jnp.einsum(
                "hqk,qhd->khd", score_grad, query_heads, preferred_element_type=jnp.float32
            )
            * score_scale
        )
    query_grad = jnp.concatenate(query_parts, axis=0)
    return (
        query_grad,
        key_grad.reshape(seq_len, col_count).astype(jnp.bfloat16),
        value_grad.reshape(seq_len, col_count).astype(jnp.bfloat16),
    )


def column_sum(values):
    return jnp.sum(values.astype(jnp.float32), axis=0, keepdims=True)


def add_tuples(first, second):
    if first is None:
        return second
    return tuple((left + right for left, right in zip(first, second)))


def pack_grads(gradients, scatter_dims, shard_count):
    pieces = []
    for gradient, scatter_dim in zip(gradients, scatter_dims):
        row_size, col_size = gradient.shape
        if scatter_dim == 0:
            pieces.append(gradient.reshape(shard_count, row_size // shard_count * col_size))
        else:
            moved = gradient.reshape(row_size, shard_count, col_size // shard_count).transpose(
                1, 0, 2
            )
            pieces.append(moved.reshape(shard_count, row_size * (col_size // shard_count)))
    return jnp.concatenate(pieces, axis=1)


def unpack_grads(flattened, gradients, scatter_dims, shard_count):
    results = []
    offset = 0
    for gradient, scatter_dim in zip(gradients, scatter_dims):
        row_size, col_size = gradient.shape
        if scatter_dim == 0:
            target = (row_size // shard_count, col_size)
        else:
            target = (row_size, col_size // shard_count)
        length = target[0] * target[1]
        results.append(flattened[0, offset : offset + length].reshape(target))
        offset = offset + length
    return tuple(results)


def shards(
    inputs,
    w_query,
    w_key,
    w_value,
    b_query,
    b_value,
    w_output,
    b_output,
    attn_gain,
    attn_shift,
    w_up,
    b_up,
    w_down,
    b_down,
    mlp_gain,
    mlp_shift,
    doc_lengths,
    out_grad,
):
    vector_rows = lax.all_gather(
        jnp.stack([b_output, attn_gain, attn_shift, b_down, mlp_gain, mlp_shift]),
        ("fsdp", "tp"),
        axis=1,
        tiled=True,
    ).astype(jnp.float32)
    out_bias = vector_rows[0]
    gain_one = vector_rows[1]
    shift_one = vector_rows[2]
    down_bias = vector_rows[3]
    gain_two = vector_rows[4]
    shift_two = vector_rows[5]
    shard_count = lax.axis_size("fsdp")
    grad_dims = (0, 0, 0, 1, 0, 1, 1, 1, 1)
    weight_sums = None
    shard_sums = None
    vector_sums = jnp.zeros(vector_rows.shape, jnp.float32)
    row_outs = []
    row_grads = []
    for batch_index in range(inputs.shape[0]):
        (
            query_full,
            key_full,
            value_full,
            output_full,
            up_full,
            down_full,
            query_bias,
            value_bias,
            up_bias,
        ) = (
            lax.all_gather(w_query, "fsdp", axis=0, tiled=True),
            lax.all_gather(w_key, "fsdp", axis=0, tiled=True),
            lax.all_gather(w_value, "fsdp", axis=0, tiled=True),
            lax.all_gather(w_output, "fsdp", axis=1, tiled=True),
            lax.all_gather(w_up, "fsdp", axis=0, tiled=True),
            lax.all_gather(w_down, "fsdp", axis=1, tiled=True),
            lax.all_gather(b_query, "fsdp", axis=1, tiled=True),
            lax.all_gather(b_value, "fsdp", axis=1, tiled=True),
            lax.all_gather(b_up, "fsdp", axis=1, tiled=True),
        )
        token_rows = inputs[batch_index]
        gathered = lax.all_gather(token_rows, "tp", axis=0, tiled=True)
        segments, places = segment_ids(doc_lengths[batch_index, 0], gathered.shape[0])
        query_rows = (
            jnp.dot(gathered, query_full, preferred_element_type=jnp.float32)
            + query_bias.astype(jnp.float32)
        ).astype(jnp.bfloat16)
        key_rows = jnp.dot(gathered, key_full, preferred_element_type=jnp.float32).astype(
            jnp.bfloat16
        )
        value_rows = (
            jnp.dot(gathered, value_full, preferred_element_type=jnp.float32)
            + value_bias.astype(jnp.float32)
        ).astype(jnp.bfloat16)
        context, logsums = attention_forward(query_rows, key_rows, value_rows, segments, places)
        attn_part = jnp.dot(context, output_full, preferred_element_type=jnp.float32)
        attn_rows = lax.psum_scatter(
            attn_part.astype(jnp.bfloat16), "tp", scatter_dimension=0, tiled=True
        ).astype(jnp.float32)
        first_out, normed_one, inverse_one = norm_forward(
            token_rows.astype(jnp.float32) + attn_rows + out_bias, gain_one, shift_one
        )
        hidden_rows = first_out.astype(jnp.bfloat16)
        hidden_full = lax.all_gather(hidden_rows, "tp", axis=0, tiled=True)
        up_pre = jnp.dot(hidden_full, up_full, preferred_element_type=jnp.float32) + up_bias.astype(
            jnp.float32
        )
        activated = jax.nn.gelu(up_pre, approximate=True).astype(jnp.bfloat16)
        mlp_rows = lax.psum_scatter(
            jnp.dot(activated, down_full, preferred_element_type=jnp.float32).astype(jnp.bfloat16),
            "tp",
            scatter_dimension=0,
            tiled=True,
        ).astype(jnp.float32)
        layer_rows, normed_two, inverse_two = norm_forward(
            hidden_rows.astype(jnp.float32) + mlp_rows + down_bias, gain_two, shift_two
        )
        row_outs.append(layer_rows.astype(jnp.bfloat16))
        upstream = out_grad[batch_index].astype(jnp.float32)
        second_grad, gain_two_grad, shift_two_grad = norm_backward(
            upstream, normed_two, inverse_two, gain_two
        )
        mixed_full = lax.all_gather(second_grad.astype(jnp.bfloat16), "tp", axis=0, tiled=True)
        down_grad = jnp.einsum(
            "sf,sd->fd", activated, mixed_full, preferred_element_type=jnp.float32
        )
        act_grad = jnp.einsum(
            "sd,fd->sf", mixed_full, down_full, preferred_element_type=jnp.float32
        )
        up_grad = jax.vjp(partial(jax.nn.gelu, approximate=True), up_pre)[1](act_grad)[0].astype(
            jnp.bfloat16
        )
        up_weight_grad = jnp.einsum(
            "sd,sf->df", hidden_full, up_grad, preferred_element_type=jnp.float32
        )
        back_rows = lax.psum_scatter(
            jnp.einsum("sf,df->sd", up_grad, up_full, preferred_element_type=jnp.float32).astype(
                jnp.bfloat16
            ),
            "tp",
            scatter_dimension=0,
            tiled=True,
        ).astype(jnp.float32)
        first_grad, gain_one_grad, shift_one_grad = norm_backward(
            second_grad + back_rows, normed_one, inverse_one, gain_one
        )
        attn_full = lax.all_gather(first_grad.astype(jnp.bfloat16), "tp", axis=0, tiled=True)
        output_grad = jnp.einsum(
            "sc,sd->cd", context, attn_full, preferred_element_type=jnp.float32
        )
        context_grad = jnp.einsum(
            "sd,cd->sc", attn_full, output_full, preferred_element_type=jnp.float32
        ).astype(jnp.bfloat16)
        query_grad, key_grad, value_grad = attention_backward(
            query_rows, key_rows, value_rows, context_grad, logsums, segments, places
        )
        query_weight_grad = jnp.einsum(
            "sd,sc->dc", gathered, query_grad, preferred_element_type=jnp.float32
        )
        key_weight_grad = jnp.einsum(
            "sd,sc->dc", gathered, key_grad, preferred_element_type=jnp.float32
        )
        value_weight_grad = jnp.einsum(
            "sd,sc->dc", gathered, value_grad, preferred_element_type=jnp.float32
        )
        token_part = (
            jnp.einsum("sc,dc->sd", query_grad, query_full, preferred_element_type=jnp.float32)
            + jnp.einsum("sc,dc->sd", key_grad, key_full, preferred_element_type=jnp.float32)
            + jnp.einsum("sc,dc->sd", value_grad, value_full, preferred_element_type=jnp.float32)
        )
        token_back = lax.psum_scatter(
            token_part.astype(jnp.bfloat16), "tp", scatter_dimension=0, tiled=True
        ).astype(jnp.float32)
        row_grads.append((first_grad + token_back).astype(jnp.bfloat16))
        vector_sums = vector_sums + jnp.stack(
            [
                jnp.sum(first_grad, axis=0),
                gain_one_grad,
                shift_one_grad,
                jnp.sum(second_grad, axis=0),
                gain_two_grad,
                shift_two_grad,
            ]
        )
        batch_grads = (
            query_weight_grad,
            key_weight_grad,
            value_weight_grad,
            output_grad,
            up_weight_grad,
            down_grad,
            column_sum(query_grad),
            column_sum(value_grad),
            column_sum(up_grad),
        )
        weight_sums = add_tuples(weight_sums, batch_grads)
    packed = pack_grads(weight_sums, grad_dims, shard_count)
    summed = lax.psum_scatter(
        packed.astype(jnp.bfloat16), "fsdp", scatter_dimension=0, tiled=True
    ).astype(jnp.float32)
    shard_sums = unpack_grads(summed, weight_sums, grad_dims, shard_count)
    vector_shards = lax.psum_scatter(vector_sums, ("fsdp", "tp"), scatter_dimension=1, tiled=True)
    return (
        jnp.stack(row_outs),
        jnp.stack(row_grads),
        shard_sums[0],
        shard_sums[1],
        shard_sums[2],
        shard_sums[6],
        shard_sums[7],
        shard_sums[3],
        vector_shards[0],
        vector_shards[1],
        vector_shards[2],
        shard_sums[4],
        shard_sums[8],
        shard_sums[5],
        vector_shards[3],
        vector_shards[4],
        vector_shards[5],
    )


def solution(mesh):
    in_specs = (
        P(None, ("fsdp", "tp"), None),
        P("fsdp", "tp"),
        P("fsdp", "tp"),
        P("fsdp", "tp"),
        P("tp", "fsdp"),
        P("tp", "fsdp"),
        P("tp", "fsdp"),
        P(("fsdp", "tp")),
        P(("fsdp", "tp")),
        P(("fsdp", "tp")),
        P("fsdp", "tp"),
        P("tp", "fsdp"),
        P("tp", "fsdp"),
        P(("fsdp", "tp")),
        P(("fsdp", "tp")),
        P(("fsdp", "tp")),
        P(None, "fsdp", None),
        P(None, ("fsdp", "tp"), None),
    )
    out_specs = (
        P(None, ("fsdp", "tp"), None),
        P(None, ("fsdp", "tp"), None),
        P("fsdp", "tp"),
        P("fsdp", "tp"),
        P("fsdp", "tp"),
        P("tp", "fsdp"),
        P("tp", "fsdp"),
        P("tp", "fsdp"),
        P(("fsdp", "tp")),
        P(("fsdp", "tp")),
        P(("fsdp", "tp")),
        P("fsdp", "tp"),
        P("tp", "fsdp"),
        P("tp", "fsdp"),
        P(("fsdp", "tp")),
        P(("fsdp", "tp")),
        P(("fsdp", "tp")),
    )
    return jax.shard_map(shards, mesh=mesh, in_specs=in_specs, out_specs=out_specs, check_vma=False)
```

profile of v0, /device:TPU:0, one launch (start us, length us, event | category | flops | bytes accessed | tf_op | source)
XLA Modules:
  0.0 1890.8 jit_solution(17971337834707523794)
XLA Ops:
  13.8 15.1 all-reduce.3
  29.4 8.8 all_gather.66
  38.2 10.8 all_gather.68
  49.0 9.9 all_gather.64
  59.0 11.0 all_gather.69
  70.1 11.1 compare_and_fusion.3
  81.2 13.7 all-gather.32.cloned.1.call-done
  99.4 76.9 %all-gather.30.cloned.1.call-done = bf16[1,2048,1024]{2,1,0:T(8,128)(2,1)} async-done(((bf16[1,512,1024]{2,1,0:T(8,128)(2,1)}), bf16[1,2048,1024]{2,1,0:T(8,128)(2,1)}) %all-gather.30.cloned.1.call-update) | async-done | bytes 4194320 | tf_op jit(solution)/shard_map/all_gather | solution.py:227
  189.8 8.1 fusion.3
  201.5 8.8 fusion.209
  217.9 8.1 fusion.2
  226.0 8.2 fusion.210
  241.9 8.1 fusion.1
  250.0 7.9 fusion.211
  265.5 8.1 fusion
  289.2 7.7 fusion.255
  296.9 8.3 fusion.4
  308.7 8.6 fusion.208
  325.0 8.3 fusion.7
  333.3 8.0 fusion.253
  341.3 8.3 fusion.6
  357.3 8.2 fusion.5
  390.4 69.6 %all-gather.2 = bf16[32,32,6]{1,2,0:T(8,128)(2,1)S(1)} all-gather(bf16[1,32,6]{1,2,0:T(8,128)(2,1)S(1)} %bitcast.572), channel_id=1, replica_groups=mesh['fsdp'=8,'tp'=4] {'fsdp','tp'}, dimensions={0}, use_global_device_ids=true | all-gather | bytes 12672 | tf_op jit(solution)/shard_map/all_gather | solution.py:185
  473.5 8.8 all_gather.73
  482.3 70.9 %all-gather.14.cloned.1.call-done = bf16[2048,1024]{1,0:T(8,128)(2,1)} async-done(((bf16[512,1024]{1,0:T(8,128)(2,1)}), bf16[2048,1024]{1,0:T(8,128)(2,1)}) %all-gather.14.cloned.1.call-update) | async-done | bytes 4194320 | tf_op jit(solution)/shard_map/all_gather | solution.py:249
  553.2 10.7 fusion.256
  563.9 17.5 all-gather.18.cloned.1.call-done
  581.4 11.8 convolution_convert_fusion.5
  593.5 70.7 %all-gather.20.cloned.1.call-done = bf16[2048,1024]{1,0:T(8,128)(2,1)} async-done(((bf16[512,1024]{1,0:T(8,128)(2,1)}), bf16[2048,1024]{1,0:T(8,128)(2,1)}) %all-gather.20.cloned.1.call-update) | async-done | bytes 4194320 | tf_op jit(solution)/shard_map/all_gather | solution.py:249
  681.7 60.1 %reduce-scatter.14.cloned.1.call-done = bf16[512,1024]{1,0:T(8,128)(2,1)} async-done(((bf16[2048,1024]{1,0:T(8,128)(2,1)}), bf16[512,1024]{1,0:T(8,128)(2,1)}) %reduce-scatter.14.cloned.1.call-update) | async-done | bytes 1048592 | tf_op jit(solution)/shard_map/reduce_scatter | solution.py:254
  743.4 77.9 %reduce-scatter.18.cloned.1.call-done = bf16[512,1024]{1,0:T(8,128)(2,1)} async-done(((bf16[2048,1024]{1,0:T(8,128)(2,1)}), bf16[512,1024]{1,0:T(8,128)(2,1)}) %reduce-scatter.18.cloned.1.call-update) | async-done | bytes 1048592 | tf_op jit(solution)/shard_map/reduce_scatter | solution.py:254
  836.2 78.1 %all-gather.22.cloned.1.call-done = bf16[2048,1024]{1,0:T(8,128)(2,1)} async-done(((bf16[512,1024]{1,0:T(8,128)(2,1)}), bf16[2048,1024]{1,0:T(8,128)(2,1)}) %all-gather.22.cloned.1.call-update) | async-done | bytes 4194320 | tf_op jit(solution)/shard_map/all_gather | solution.py:268
  914.3 10.8 fusion.258
  925.1 69.9 %all-gather.26.cloned.1.call-done = bf16[2048,1024]{1,0:T(8,128)(2,1)} async-done(((bf16[512,1024]{1,0:T(8,128)(2,1)}), bf16[2048,1024]{1,0:T(8,128)(2,1)}) %all-gather.26.cloned.1.call-update) | async-done | bytes 4194320 | tf_op jit(solution)/shard_map/all_gather | solution.py:268
  995.0 21.9 %convert_reduce_fusion = (f32[1024]{0:T(1024)S(1)}, bf16[2048,1024]{1,0:T(8,128)(2,1)}, f32[1024]{0:T(1024)S(1)}, bf16[2048,1024]{1,0:T(8,128)(2,1)S(1)}) fusion(f32[2048,1024]{1,0:T(8,128)} %copy-done.179, f32[1024]{0:T(1024)S(1)} %bitcast.575, f32[2048,1024]{1,0:T(8,128)} %fusion.258, f32[2048,1024]{1,0:T(8,128)} %fusion.256, ...), kind=kOutput, calls=%fused_computation.90 | convolution fusion | flops 4391434240 | bytes 39858176 | tf_op jit(solution)/shard_map/sd,fd->sf/dot_general | solution.py:272
  1025.6 9.4 convolution_convert_fusion.2
  1035.0 65.7 %reduce-scatter.20.cloned.1.call-done = bf16[512,1024]{1,0:T(8,128)(2,1)} async-done(((bf16[2048,1024]{1,0:T(8,128)(2,1)}), bf16[512,1024]{1,0:T(8,128)(2,1)}) %reduce-scatter.20.cloned.1.call-update) | async-done | bytes 1048592 | tf_op jit(solution)/shard_map/reduce_scatter | solution.py:281
  1100.7 79.4 %reduce-scatter.24.cloned.1.call-done = bf16[512,1024]{1,0:T(8,128)(2,1)} async-done(((bf16[2048,1024]{1,0:T(8,128)(2,1)}), bf16[512,1024]{1,0:T(8,128)(2,1)}) %reduce-scatter.24.cloned.1.call-update) | async-done | bytes 1048592 | tf_op jit(solution)/shard_map/reduce_scatter | solution.py:281
  1196.9 9.4 fusion.227
  1206.3 8.8 add_convert_fusion.2
  1218.0 7.8 fusion.263
  1234.7 38.7 %all-gather.24.cloned.1.call-done = bf16[2048,1024]{1,0:T(8,128)(2,1)} async-done(((bf16[512,1024]{1,0:T(8,128)(2,1)}), bf16[2048,1024]{1,0:T(8,128)(2,1)}) %all-gather.24.cloned.1.call-update) | async-done | bytes 4194320 | tf_op jit(solution)/shard_map/all_gather | solution.py:292
  1276.9 12.6 multiply_reduce_fusion.7
  1289.6 15.9 multiply_convert_fusion.7
  1305.5 7.7 fusion.197
  1323.6 8.4 multiply_reduce_fusion.6
  1339.5 13.4 multiply_reduce_fusion.5
  1357.2 8.3 multiply_reduce_fusion.4
  1370.0 11.2 multiply_reduce_fusion.3
  1381.2 15.8 multiply_convert_fusion.3
  1415.1 8.7 multiply_reduce_fusion.2
  1423.8 8.8 fusion.32
  1432.6 13.6 multiply_reduce_fusion.1
  1450.3 8.8 multiply_reduce_fusion
  1465.1 12.5 convert_reduce_fusion.4
  1490.1 12.0 multiply_convert_fusion.6
  1507.2 12.3 multiply_convert_fusion.5
  1525.8 7.7 multiply_convert_fusion.4
  1539.5 12.1 multiply_convert_fusion.2
  1556.6 12.3 multiply_convert_fusion.1
  1575.2 8.2 multiply_convert_fusion
  1641.7 79.9 %all-reduce.6.cloned.1.call-done = bf16[8,393408]{1,0:T(8,128)(2,1)} async-done(((bf16[8,393408]{1,0:T(8,128)(2,1)}), bf16[8,393408]{1,0:T(8,128)(2,1)}) %all-reduce.6.cloned.1.call-update) | async-done | bytes 6294544
  1735.7 64.9 %reduce-scatter.22.cloned.1.call-done = bf16[512,1024]{1,0:T(8,128)(2,1)} async-done(((bf16[2048,1024]{1,0:T(8,128)(2,1)}), bf16[512,1024]{1,0:T(8,128)(2,1)}) %reduce-scatter.22.cloned.1.call-update) | async-done | bytes 1048592 | tf_op jit(solution)/shard_map/reduce_scatter | solution.py:316
  1802.8 77.4 %reduce-scatter.26.cloned.1.call-done = bf16[512,1024]{1,0:T(8,128)(2,1)} async-done(((bf16[2048,1024]{1,0:T(8,128)(2,1)}), bf16[512,1024]{1,0:T(8,128)(2,1)}) %reduce-scatter.26.cloned.1.call-update) | async-done | bytes 1048592 | tf_op jit(solution)/shard_map/reduce_scatter | solution.py:316
  (649 shorter events, 369.4 us)
Async XLA Ops:
  8.1 20.9 %copy-start.143 = (s32[2,1,8]{2,1,0:T(1,128)S(1)}, s32[2,1,8]{2,1,0:T(1,128)}, u32[]{:S(2)}) copy-start(s32[2,1,8]{2,1,0:T(1,128)} %param.34) | copy-start | bytes 196
  8.1 21.3 %copy-start.114 = (bf16[128,256]{1,0:T(8,128)(2,1)S(1)}, bf16[128,256]{1,0:T(8,128)(2,1)}, u32[]{:S(2)}) copy-start(bf16[128,256]{1,0:T(8,128)(2,1)} %param.19) | copy-start | bytes 196612
  8.1 30.1 %copy-start.115 = (bf16[128,256]{1,0:T(8,128)(2,1)S(1)}, bf16[128,256]{1,0:T(8,128)(2,1)}, u32[]{:S(2)}) copy-start(bf16[128,256]{1,0:T(8,128)(2,1)} %param.20) | copy-start | bytes 196612
  8.1 41.0 %copy-start.116 = (bf16[128,256]{1,0:T(8,128)(2,1)S(1)}, bf16[128,256]{1,0:T(8,128)(2,1)}, u32[]{:S(2)}) copy-start(bf16[128,256]{1,0:T(8,128)(2,1)} %param.21) | copy-start | bytes 196612
  8.1 50.9 %copy-start.117 = (bf16[256,128]{1,0:T(8,128)(2,1)S(1)}, bf16[256,128]{1,0:T(8,128)(2,1)}, u32[]{:S(2)}) copy-start(bf16[256,128]{1,0:T(8,128)(2,1)} %param.24) | copy-start | bytes 196612
  8.1 86.8 %all-gather.32.cloned.1.call-start = ((), (), s32[]{:S(2)}) async-start(), calls=%async_computation.26 | async-start | bytes 5242880 | tf_op jit(solution)/shard_map/all_gather | solution.py:227
  11.3 165.0 %all-gather.30.cloned.1.call-start = ((), (), s32[]{:S(2)}) async-start(), calls=%async_computation.25 | async-start | bytes 5242880 | tf_op jit(solution)/shard_map/all_gather | solution.py:227
  12.0 448.1 %reduce-scatter.12.cloned.1.call-start = ((), (), s32[]{:S(2)}) async-start(), calls=%async_computation.9 | async-start | bytes 5242880 | tf_op jit(solution)/shard_map/reduce_scatter | solution.py:242
  38.2 138.1 %copy-start.47 = (bf16[1024,256]{1,0:T(8,128)(2,1)}, bf16[1024,256]{1,0:T(8,128)(2,1)S(1)}, u32[]{:S(2)}) copy-start(bf16[1024,256]{1,0:T(8,128)(2,1)S(1)} %all_gather.66) | copy-start | bytes 1572868
  180.8 29.5 %copy-start.66 = (bf16[512,256]{0,1:T(8,128)(2,1)}, bf16[512,256]{0,1:T(8,128)(2,1)S(1)}, u32[]{:S(2)}) copy-start(bf16[512,256]{0,1:T(8,128)(2,1)S(1)} %get-tuple-element.87) | copy-start | bytes 786436
  182.1 75.8 %copy-start = (bf16[2048,256]{0,1:T(8,128)(2,1)}, bf16[2048,256]{0,1:T(8,128)(2,1)S(1)}, u32[]{:S(2)}) copy-start(bf16[2048,256]{0,1:T(8,128)(2,1)S(1)} %fusion.148) | copy-start | bytes 3145732
  201.5 72.2 %copy-start.7 = (bf16[2048,256]{0,1:T(8,128)(2,1)}, bf16[2048,256]{0,1:T(8,128)(2,1)S(1)}, u32[]{:S(2)}) copy-start(bf16[2048,256]{0,1:T(8,128)(2,1)S(1)} %fusion.143) | copy-start | bytes 3145732
  257.9 23.4 %copy-start.167 = (bf16[4,64,512]{2,1,0:T(8,128)(2,1)}, bf16[4,64,512]{2,1,0:T(8,128)(2,1)S(1)}, u32[]{:S(2)}) copy-start(bf16[4,64,512]{2,1,0:T(8,128)(2,1)S(1)} %fusion.211) | copy-start | bytes 786436
  284.7 181.9 %reduce-scatter.16.cloned.1.call-start = ((), (), s32[]{:S(2)}) async-start(), calls=%async_computation.14 | async-start | bytes 5242880 | tf_op jit(solution)/shard_map/reduce_scatter | solution.py:242
  289.2 60.5 %copy-start.3 = (bf16[2048,256]{0,1:T(8,128)(2,1)}, bf16[2048,256]{0,1:T(8,128)(2,1)S(1)}, u32[]{:S(2)}) copy-start(bf16[2048,256]{0,1:T(8,128)(2,1)S(1)} %fusion.151) | copy-start | bytes 3145732
  308.7 72.2 %copy-start.9 = (bf16[2048,256]{0,1:T(8,128)(2,1)}, bf16[2048,256]{0,1:T(8,128)(2,1)S(1)}, u32[]{:S(2)}) copy-start(bf16[2048,256]{0,1:T(8,128)(2,1)S(1)} %fusion.137) | copy-start | bytes 3145732
  325.0 40.6 %copy-start.108 = (f32[4,512]{1,0:T(4,128)}, f32[4,512]{1,0:T(4,128)S(1)}, u32[]{:S(2)}) copy-start(f32[4,512]{1,0:T(4,128)S(1)} %get-tuple-element.139) | copy-start | bytes 24580
  333.3 32.2 %copy-start.128 = (f32[4,512]{1,0:T(4,128)}, f32[4,512]{1,0:T(4,128)S(1)}, u32[]{:S(2)}) copy-start(f32[4,512]{1,0:T(4,128)S(1)} %fusion.7) | copy-start | bytes 24580
  341.3 31.9 %copy-start.110 = (f32[4,512]{1,0:T(4,128)}, f32[4,512]{1,0:T(4,128)S(1)}, u32[]{:S(2)}) copy-start(f32[4,512]{1,0:T(4,128)S(1)} %get-tuple-element.141) | copy-start | bytes 24580
  349.6 23.6 %copy-start.130 = (f32[4,512]{1,0:T(4,128)}, f32[4,512]{1,0:T(4,128)S(1)}, u32[]{:S(2)}) copy-start(f32[4,512]{1,0:T(4,128)S(1)} %fusion.6) | copy-start | bytes 24580
  357.3 23.6 %copy-start.112 = (f32[4,512]{1,0:T(4,128)}, f32[4,512]{1,0:T(4,128)S(1)}, u32[]{:S(2)}) copy-start(f32[4,512]{1,0:T(4,128)S(1)} %get-tuple-element.143) | copy-start | bytes 24580
  389.6 70.5 %copy-start.6 = (bf16[2,512,1024]{2,1,0:T(8,128)(2,1)S(1)}, bf16[2,512,1024]{2,1,0:T(8,128)(2,1)}, u32[]{:S(2)}) copy-start(bf16[2,512,1024]{2,1,0:T(8,128)(2,1)} %param.18) | copy-start | bytes 6291460
  389.7 92.6 %all-gather.16.cloned.1.call-start = ((), (), s32[]{:S(2)}) async-start(), calls=%async_computation.11 | async-start | bytes 2359296 | tf_op jit(solution)/shard_map/all_gather | solution.py:220
  390.2 162.9 %all-gather.14.cloned.1.call-start = ((), (), s32[]{:S(2)}) async-start(), calls=%async_computation.10 | async-start | bytes 5242880 | tf_op jit(solution)/shard_map/all_gather | solution.py:249
  472.2 109.3 %all-gather.18.cloned.1.call-start = ((), (), s32[]{:S(2)}) async-start(), calls=%async_computation.12 | async-start | bytes 2359296 | tf_op jit(solution)/shard_map/all_gather | solution.py:221
  472.7 191.5 %all-gather.20.cloned.1.call-start = ((), (), s32[]{:S(2)}) async-start(), calls=%async_computation.15 | async-start | bytes 5242880 | tf_op jit(solution)/shard_map/all_gather | solution.py:249
  473.5 268.3 %reduce-scatter.14.cloned.1.call-start = ((), (), s32[]{:S(2)}) async-start(), calls=%async_computation.13 | async-start | bytes 5242880 | tf_op jit(solution)/shard_map/reduce_scatter | solution.py:254
  593.2 228.1 %reduce-scatter.18.cloned.1.call-start = ((), (), s32[]{:S(2)}) async-start(), calls=%async_computation.16 | async-start | bytes 5242880 | tf_op jit(solution)/shard_map/reduce_scatter | solution.py:254
  681.6 60.1 %copy-start.11 = (bf16[512,1024]{1,0:T(8,128)(2,1)S(1)}, bf16[512,1024]{1,0:T(8,128)(2,1)}, u32[]{:S(2)}) copy-start(bf16[512,1024]{1,0:T(8,128)(2,1)} %get-tuple-element.66) | copy-start | bytes 3145732
  681.6 232.7 %all-gather.22.cloned.1.call-start = ((), (), s32[]{:S(2)}) async-start(), calls=%async_computation.17 | async-start | bytes 5242880 | tf_op jit(solution)/shard_map/all_gather | solution.py:268
  833.0 162.1 %all-gather.26.cloned.1.call-start = ((), (), s32[]{:S(2)}) async-start(), calls=%async_computation.21 | async-start | bytes 5242880 | tf_op jit(solution)/shard_map/all_gather | solution.py:268
  835.8 264.9 %reduce-scatter.20.cloned.1.call-start = ((), (), s32[]{:S(2)}) async-start(), calls=%async_computation.18 | async-start | bytes 5242880 | tf_op jit(solution)/shard_map/reduce_scatter | solution.py:281
  995.0 23.9 %copy-start.159 = (bf16[1024,1024]{1,0:T(8,128)(2,1)S(1)}, bf16[1024,1024]{1,0:T(8,128)(2,1)}, u32[]{:S(2)}) copy-start(bf16[1024,1024]{1,0:T(8,128)(2,1)} %all-gather.16.cloned.1.call-done) | copy-start | bytes 6291460
  1025.3 154.7 %reduce-scatter.24.cloned.1.call-start = ((), (), s32[]{:S(2)}) async-start(), calls=%async_computation.22 | async-start | bytes 5242880 | tf_op jit(solution)/shard_map/reduce_scatter | solution.py:281
  1034.9 145.2 %copy-start.15 = (bf16[512,1024]{1,0:T(8,128)(2,1)S(1)}, bf16[512,1024]{1,0:T(8,128)(2,1)}, u32[]{:S(2)}) copy-start(bf16[512,1024]{1,0:T(8,128)(2,1)} %reduce-scatter.12.cloned.1.call-done) | copy-start | bytes 3145732
  1035.0 238.4 %all-gather.24.cloned.1.call-start = ((), (), s32[]{:S(2)}) async-start(), calls=%async_computation.19 | async-start | bytes 5242880 | tf_op jit(solution)/shard_map/all_gather | solution.py:292
  1191.5 174.0 %all-gather.28.cloned.1.call-start = ((), (), s32[]{:S(2)}) async-start(), calls=%async_computation.23 | async-start | bytes 5242880 | tf_op jit(solution)/shard_map/all_gather | solution.py:292
  1195.3 161.9 %copy-start.90 = (f32[4,512]{1,0:T(4,128)}, f32[4,512]{1,0:T(4,128)S(1)}, u32[]{:S(2)}) copy-start(f32[4,512]{1,0:T(4,128)S(1)} %log_add_fusion.4) | copy-start | bytes 24580
  1196.5 433.7 %reduce-scatter.28.cloned.1.call-start = ((), (), s32[]{:S(2)}) async-start(), calls=%async_computation.27 | async-start | bytes 540672
  1196.8 142.7 %copy-start.92 = (f32[4,512]{1,0:T(4,128)}, f32[4,512]{1,0:T(4,128)S(1)}, u32[]{:S(2)}) copy-start(f32[4,512]{1,0:T(4,128)S(1)} %log_add_fusion.5) | copy-start | bytes 24580
  1196.8 126.8 %copy-start.94 = (f32[4,512]{1,0:T(4,128)}, f32[4,512]{1,0:T(4,128)S(1)}, u32[]{:S(2)}) copy-start(f32[4,512]{1,0:T(4,128)S(1)} %log_add_fusion.6) | copy-start | bytes 24580
  1196.9 92.7 %copy-start.96 = (f32[4,512]{1,0:T(4,128)}, f32[4,512]{1,0:T(4,128)S(1)}, u32[]{:S(2)}) copy-start(f32[4,512]{1,0:T(4,128)S(1)} %log_add_fusion.7) | copy-start | bytes 24580
  1230.6 42.8 %copy-start.86 = (bf16[256,1024]{1,0:T(8,128)(2,1)S(1)}, bf16[256,1024]{1,0:T(8,128)(2,1)}, u32[]{:S(2)}) copy-start(bf16[256,1024]{1,0:T(8,128)(2,1)} %all_gather.69) | copy-start | bytes 1572868
  1234.6 42.3 %copy-start.8 = (bf16[2048,256]{0,1:T(8,128)(2,1)S(1)}, bf16[2048,256]{0,1:T(8,128)(2,1)}, u32[]{:S(2)}) copy-start(bf16[2048,256]{0,1:T(8,128)(2,1)} %copy-done.7) | copy-start | bytes 3145732
  1234.6 487.0 %all-reduce.6.cloned.1.call-start = ((), (), s32[]{:S(2)}) async-start(), calls=%async_computation.28 | async-start | bytes 12591104
  1289.6 30.0 %slice-start.16 = ((s8[16777216]{0:T(1024)(128)(4,1)}), s8[4194304]{0:T(1024)(128)(4,1)S(1)}, s32[]{:S(2)}) async-start(s8[16777216]{0:T(1024)(128)(4,1)} %bitcast.431), calls=%async_computation.45 | async-start | bytes 8388608
  1289.6 30.0 %slice-start.17 = ((s8[16777216]{0:T(1024)(128)(4,1)}), s8[4194304]{0:T(1024)(128)(4,1)S(1)}, s32[]{:S(2)}) async-start(s8[16777216]{0:T(1024)(128)(4,1)} %bitcast.431), calls=%async_computation.46 | async-start | bytes 8388608
  1289.6 30.0 %slice-start.18 = ((s8[16777216]{0:T(1024)(128)(4,1)}), s8[4194304]{0:T(1024)(128)(4,1)S(1)}, s32[]{:S(2)}) async-start(s8[16777216]{0:T(1024)(128)(4,1)} %bitcast.431), calls=%async_computation.47 | async-start | bytes 8388608
  1332.1 20.9 %slice-start = ((s8[16777216]{0:T(1024)(128)(4,1)}), s8[4194304]{0:T(1024)(128)(4,1)S(1)}, s32[]{:S(2)}) async-start(s8[16777216]{0:T(1024)(128)(4,1)} %bitcast.423), calls=%async_computation.29 | async-start | bytes 8388608
  1332.1 20.9 %slice-start.1 = ((s8[16777216]{0:T(1024)(128)(4,1)}), s8[4194304]{0:T(1024)(128)(4,1)S(1)}, s32[]{:S(2)}) async-start(s8[16777216]{0:T(1024)(128)(4,1)} %bitcast.423), calls=%async_computation.30 | async-start | bytes 8388608
  1381.1 29.9 %slice-start.24 = ((s8[16777216]{0:T(1024)(128)(4,1)}), s8[4194304]{0:T(1024)(128)(4,1)S(1)}, s32[]{:S(2)}) async-start(s8[16777216]{0:T(1024)(128)(4,1)} %bitcast.435), calls=%async_computation.53 | async-start | bytes 8388608
  1381.1 29.9 %slice-start.25 = ((s8[16777216]{0:T(1024)(128)(4,1)}), s8[4194304]{0:T(1024)(128)(4,1)S(1)}, s32[]{:S(2)}) async-start(s8[16777216]{0:T(1024)(128)(4,1)} %bitcast.435), calls=%async_computation.54 | async-start | bytes 8388608
  1381.2 29.9 %slice-start.26 = ((s8[16777216]{0:T(1024)(128)(4,1)}), s8[4194304]{0:T(1024)(128)(4,1)S(1)}, s32[]{:S(2)}) async-start(s8[16777216]{0:T(1024)(128)(4,1)} %bitcast.435), calls=%async_computation.55 | async-start | bytes 8388608
  1423.8 22.4 %slice-start.8 = ((s8[16777216]{0:T(1024)(128)(4,1)}), s8[4194304]{0:T(1024)(128)(4,1)S(1)}, s32[]{:S(2)}) async-start(s8[16777216]{0:T(1024)(128)(4,1)} %bitcast.427), calls=%async_computation.37 | async-start | bytes 8388608
  1423.8 22.4 %slice-start.9 = ((s8[16777216]{0:T(1024)(128)(4,1)}), s8[4194304]{0:T(1024)(128)(4,1)S(1)}, s32[]{:S(2)}) async-start(s8[16777216]{0:T(1024)(128)(4,1)} %bitcast.427), calls=%async_computation.38 | async-start | bytes 8388608
  1507.2 18.6 slice-start.4
  1507.2 18.6 slice-start.5
  1507.2 18.6 slice-start.6
  1556.6 18.6 slice-start.12
  1556.6 18.6 slice-start.13
  1556.6 18.6 slice-start.14
  1618.9 181.7 %reduce-scatter.22.cloned.1.call-start = ((), (), s32[]{:S(2)}) async-start(), calls=%async_computation.20 | async-start | bytes 5242880 | tf_op jit(solution)/shard_map/reduce_scatter | solution.py:316
  1627.0 253.2 %reduce-scatter.26.cloned.1.call-start = ((), (), s32[]{:S(2)}) async-start(), calls=%async_computation.24 | async-start | bytes 5242880 | tf_op jit(solution)/shard_map/reduce_scatter | solution.py:316
  1728.9 151.2 %copy-start.19 = (f32[512,1024]{1,0:T(8,128)S(1)}, f32[512,1024]{1,0:T(8,128)}, u32[]{:S(2)}) copy-start(f32[512,1024]{1,0:T(8,128)} %get-tuple-element.69) | copy-start | bytes 6291460
  (168 other events, 1060.3 us)
Sparse Core Ops, SparseCore 0:
  11.4 83.4 all-gather.31
  97.0 79.2 all-gather.29
  284.8 75.2 reduce-scatter.11
  389.8 76.7 reduce-scatter.15
  833.1 81.2 all-gather.21
  915.8 79.2 all-gather.25
  1191.6 81.7 all-gather.23
  1275.5 79.9 all-gather.27
Sparse Core Ops, SparseCore 1:
  392.0 26.4 all-gather.15
  472.2 80.9 all-gather.13
  554.9 26.4 all-gather.17
  583.6 80.6 all-gather.19
  666.5 75.2 reduce-scatter.13
  744.1 77.2 reduce-scatter.17
  1025.4 75.2 reduce-scatter.19
  1102.8 77.2 reduce-scatter.23
  1234.7 218.7 reduce-scatter.27
  1619.0 102.6 all-reduce.5
  1723.8 76.7 reduce-scatter.21
  1802.9 77.2 reduce-scatter.25
where the time goes:
time: 1900 us; the launch traced here: 1890 us
  waiting for transfers between devices  949 us (50%)
  matrix products  500 us (26%)
  other arithmetic  226 us (12%)
  blocking collectives  134 us (7%)
  local copies, waits for them, and re-layouts  61.2 us (3%)
  between operations  19.2 us (1%)
    all_gather x2, waiting for transfers between devices, shards(): lax.all_gather(second_grad.astype(jnp.bfloat16), 'tp', axis=0, tiled=True)  148 us
    reduce_scatter x2, waiting for transfers between devices, shards(): lax.psum_scatter(jnp.einsum('sf,df->sd', up_grad, up_full, preferred_elem...  145 us
    reduce_scatter x2, waiting for transfers between devices, shards(): lax.psum_scatter(token_part.astype(jnp.bfloat16), 'tp', scatter_dimension...  142 us
    all_gather x2, waiting for transfers between devices, shards(): hidden_full = lax.all_gather(hidden_rows, 'tp', axis=0, tiled=True)  142 us
    reduce_scatter x2, waiting for transfers between devices, shards(): lax.psum_scatter(jnp.dot(activated, down_full, preferred_element_type=jnp...  138 us
    convert_element_type x8, other arithmetic, attention_backward(): score_grad = (attn_probs * (prob_grad - row_delta)).astype(jnp.bfloat16)  96.3 us
    all_gather x2, waiting for transfers between devices, shards(): gathered = lax.all_gather(token_rows, 'tp', axis=0, tiled=True)  90.6 us
    dot_general x8, matrix products, attention_backward(): jnp.einsum('qhd,khd->hqk', grad_heads, value_heads, preferred_element_typ...  85 us
  transfers between devices with their start and end apart: 20, of which 16 were waited for; matrix products, arithmetic and copies ran while one was open for 32% of the time, Pallas kernels for 0%

commit v1 on v0

--- a/solution.py
+++ b/solution.py
@@ -3,6 +3,8 @@
 import jax
 import jax.numpy as jnp
 from jax import lax
+from jax.experimental import pallas as pl
+from jax.experimental.pallas import tpu as pltpu
 from jax.sharding import PartitionSpec as P
 
 HEAD_DIM = 64
@@ -366,6 +368,834 @@
     )
 
 
+AXES = ("fsdp", "tp")
+TN = (((0,), (0,)), ((), ()))
+NT = (((1,), (1,)), ((), ()))
+VMEM_LIMIT = 60 * 1024 * 1024
+ANY = pl.BlockSpec(memory_space=pl.ANY)
+STEPS = (0, 2, 1, 3)
+
+
+def params(**kwargs):
+    return pltpu.CompilerParams(vmem_limit_bytes=VMEM_LIMIT, **kwargs)
+
+
+def dot(left, right, dims=(((1,), (0,)), ((), ()))):
+    return lax.dot_general(left, right, dims, preferred_element_type=jnp.float32)
+
+
+def place_of(step):
+    return (step % 2) * 2 + step // 2
+
+
+def swap(values, fsdp_bits, tp_bits):
+    fsdp_size, tp_size = lax.axis_size("fsdp"), lax.axis_size("tp")
+    pairs = [
+        (f * tp_size + t, (f ^ fsdp_bits) * tp_size + (t ^ tp_bits))
+        for f in range(fsdp_size)
+        for t in range(tp_size)
+    ]
+    return lax.ppermute(values, AXES, pairs)
+
+
+def home_pairs(second):
+    pairs = []
+    for group in range(lax.axis_size("fsdp") // 2):
+        for core in range(2):
+            for t in range(4):
+                micro = (t % 2) ^ second
+                pairs.append(((group * 2 + core) * 4 + t, (group * 2 + t // 2) * 4 + micro * 2 + core))
+    return pairs
+
+
+def to_sequences(rows, t):
+    odd = t % 2
+    first = lax.dynamic_index_in_dim(rows, odd, 0, keepdims=False)
+    second = lax.dynamic_index_in_dim(rows, 1 - odd, 0, keepdims=False)
+    return (lax.ppermute(first, AXES, home_pairs(0)), lax.ppermute(second, AXES, home_pairs(1)))
+
+
+def to_homes(rows, t):
+    micro = t // 2
+    halves = rows.reshape(2, rows.shape[0] // 2, rows.shape[1])
+    first = lax.dynamic_index_in_dim(halves, micro, 0, keepdims=False)
+    second = lax.dynamic_index_in_dim(halves, 1 - micro, 0, keepdims=False)
+    first = lax.ppermute(first, AXES, [(b, a) for a, b in home_pairs(0)])
+    second = lax.ppermute(second, AXES, [(b, a) for a, b in home_pairs(1)])
+    odd = t % 2
+    return jnp.where(odd == 0, jnp.stack([first, second]), jnp.stack([second, first]))
+
+
+def gather_pieces(shard, first_bits, second_bits):
+    pair = jnp.stack([shard, swap(shard, 0, 2)])
+    quad = jnp.concatenate([pair, swap(pair, 0, 1)])
+    pieces = {0: quad}
+    pieces[first_bits] = swap(quad, first_bits, 0)
+    pieces[second_bits] = swap(quad, second_bits, 0)
+    pieces[6] = swap(pieces[first_bits], second_bits, 0)
+    for offset in (0, first_bits, second_bits, 6):
+        pieces[offset + 1] = swap(pieces[offset], 1, 0)
+    return [pieces[offset] for offset in range(8)]
+
+
+def qkv_kernel(info, *refs):
+    pieces, tokens, biases = refs[:8], refs[8:12], refs[12]
+    rows_ref, weight_ref, query_ref, key_ref, value_ref = refs[13:18]
+    row_sems, weight_sems = refs[18:]
+    f, t, core, micro = info[0], info[1], info[2], info[3]
+    copies = []
+    for offset in range(8):
+        block = f ^ offset
+        for j in range(2):
+            place = place_of(t ^ (2 * core + j))
+            for which in range(3):
+                copies.append(
+                    pltpu.make_async_copy(
+                        pieces[offset].at[place, pl.ds(which * 128, 128), :],
+                        weight_ref.at[which, pl.ds(pl.multiple_of(block * 128, 128), 128), pl.ds(j * 256, 256)],
+                        weight_sems.at[len(copies)],
+                    )
+                )
+    for k in range(4):
+        quarter = (k // 2) * 2 + (micro if k % 2 == 0 else 1 - micro)
+        copies.append(
+            pltpu.make_async_copy(
+                tokens[k], rows_ref.at[pl.ds(pl.multiple_of(quarter * 512, 512), 512), :], row_sems.at[k]
+            )
+        )
+    for copy in copies:
+        copy.start()
+    for copy in copies:
+        copy.wait()
+    for block in range(8):
+        span = pl.ds(block * 256, 256)
+        rows = rows_ref[span, :]
+        query_ref[span, :] = (
+            (dot(rows, weight_ref[0]) + biases[0:1, :]).astype(jnp.bfloat16).astype(jnp.float32)
+            * HEAD_DIM ** (-0.5)
+        ).astype(jnp.bfloat16)
+        key_ref[span, :] = dot(rows, weight_ref[1]).astype(jnp.bfloat16)
+        value_ref[span, :] = (dot(rows, weight_ref[2]) + biases[1:2, :]).astype(jnp.bfloat16)
+
+
+def project(info, pieces, tokens, biases):
+    head_rows = jax.ShapeDtypeStruct((2048, 512), jnp.bfloat16)
+    whole = pl.BlockSpec(memory_space=pltpu.VMEM)
+    return pl.pallas_call(
+        qkv_kernel,
+        out_shape=(
+            jax.ShapeDtypeStruct((2048, 1024), jnp.bfloat16),
+            jax.ShapeDtypeStruct((3, 1024, 512), jnp.bfloat16),
+            head_rows,
+            head_rows,
+            head_rows,
+        ),
+        grid_spec=pltpu.PrefetchScalarGridSpec(
+            num_scalar_prefetch=1,
+            grid=(),
+            in_specs=[ANY] * 12 + [whole],
+            out_specs=[whole] * 5,
+            scratch_shapes=[pltpu.SemaphoreType.DMA((4,)), pltpu.SemaphoreType.DMA((48,))],
+        ),
+        compiler_params=params(),
+        name="qkv",
+    )(info, *pieces, *tokens, biases)
+
+
+def head_mask(rows):
+    return lax.broadcasted_iota(jnp.int32, (rows, 128), 1) < HEAD_DIM
+
+
+def split_heads(pair):
+    low = head_mask(pair.shape[0])
+    zero = jnp.zeros_like(pair)
+    return (jnp.where(low, pair, zero), jnp.where(low, zero, pair))
+
+
+def three_loops(info, block, body, carry):
+    base = 8 + block * 4
+    lo, hi, full_lo, full_hi = info[base], info[base + 1], info[base + 2], info[base + 3]
+    carry = lax.fori_loop(lo, full_lo, partial(body, True), carry)
+    carry = lax.fori_loop(full_lo, full_hi, partial(body, False), carry)
+    return lax.fori_loop(full_hi, hi, partial(body, True), carry)
+
+
+def key_span(info, block):
+    return pl.ds(pl.multiple_of((block ^ (info[2] * 4)) * 256, 256), 256)
+
+
+def masked(scores, bounds_ref, block):
+    places = block * 256 + lax.broadcasted_iota(jnp.int32, scores.shape, 0)
+    allowed = (places >= bounds_ref[0:1, :]) & (places < bounds_ref[1:2, :])
+    return jnp.where(allowed, scores, MASKED)
+
+
+def attend_kernel(first_block, info, query_ref, key_ref, value_ref, bounds_ref, context_ref, lse_ref, turned):
+    step = pl.program_id(1)
+
+    @pl.when(step == 0)
+    def _():
+        turned[...] = value_ref[...].T
+
+    queries = split_heads(query_ref[...])
+
+    def body(use_mask, block, carry):
+        span = key_span(info, block)
+        keys = key_ref[span, :]
+        out = []
+        for h in range(2):
+            top, total, context = carry[h]
+            scores = dot(keys, queries[h], NT)
+            if use_mask:
+                scores = masked(scores, bounds_ref, block)
+            new_top = jnp.maximum(top, jnp.max(scores, axis=0, keepdims=True))
+            decay = jnp.exp(top - new_top)
+            exponent = jnp.exp(scores - new_top)
+            total = total * decay + jnp.sum(exponent, axis=0, keepdims=True)
+            context = context * decay + dot(
+                turned[h * HEAD_DIM : (h + 1) * HEAD_DIM, span], exponent.astype(jnp.bfloat16)
+            )
+            out.append((new_top, total, context))
+        return tuple(out)
+
+    start = (
+        jnp.full((1, 256), 2 * MASKED, jnp.float32),
+        jnp.zeros((1, 256), jnp.float32),
+        jnp.zeros((HEAD_DIM, 256), jnp.float32),
+    )
+    heads = three_loops(info, first_block + step, body, (start, start))
+    context_ref[...] = jnp.concatenate(
+        [context / total for _, total, context in heads], axis=0
+    ).T.astype(jnp.bfloat16)
+    lse_ref[0, 0:1, :] = heads[0][0] + jnp.log(heads[0][1])
+    lse_ref[0, 1:2, :] = heads[1][0] + jnp.log(heads[1][1])
+
+
+def attend(info, queries, keys, values, bounds, half):
+    first_block = half * 4
+    return pl.pallas_call(
+        partial(attend_kernel, first_block),
+        out_shape=(
+            jax.ShapeDtypeStruct((1024, 512), jnp.bfloat16),
+            jax.ShapeDtypeStruct((4, 8, 1024), jnp.float32),
+        ),
+        grid_spec=pltpu.PrefetchScalarGridSpec(
+            num_scalar_prefetch=1,
+            grid=(4, 4),
+            in_specs=[
+                pl.BlockSpec((256, 128), lambda p, i, s: (first_block + i, p)),
+                pl.BlockSpec((2048, 128), lambda p, i, s: (0, p)),
+                pl.BlockSpec((2048, 128), lambda p, i, s: (0, p)),
+                pl.BlockSpec((8, 256), lambda p, i, s: (0, first_block + i)),
+            ],
+            out_specs=[
+                pl.BlockSpec((256, 128), lambda p, i, s: (i, p)),
+                pl.BlockSpec((1, 8, 256), lambda p, i, s: (p, 0, i)),
+            ],
+            scratch_shapes=[pltpu.VMEM((128, 2048), jnp.bfloat16)],
+        ),
+        compiler_params=params(),
+        name="attend",
+    )(info, queries, keys, values, bounds)
+
+
+def attend_back_kernel(
+    info, query_ref, key_ref, value_ref, bounds_ref,
+    context_own, context_other, grad_own, grad_other, lse_own, lse_other,
+    query_grad, key_grad, value_grad, query_sum, value_sum,
+    turned, key_total, value_total,
+):
+    step = pl.program_id(1)
+
+    @pl.when(step == 0)
+    def _():
+        turned[...] = key_ref[...].T
+        key_total[...] = jnp.zeros_like(key_total)
+        value_total[...] = jnp.zeros_like(value_total)
+        query_sum[...] = jnp.zeros_like(query_sum)
+
+    own = step < 4
+    context = jnp.where(own, context_own[...], context_other[...])
+    grad_pair = jnp.where(own, grad_own[...], grad_other[...])
+    lse = jnp.where(own, lse_own[0], lse_other[0])
+    product = (context.astype(jnp.float32) * grad_pair.astype(jnp.float32)).T
+    queries = split_heads(query_ref[...])
+    grads = split_heads(grad_pair)
+    query_stack = jnp.concatenate(queries, axis=0)
+    grad_stack = jnp.concatenate(grads, axis=0)
+    deltas = [
+        jnp.sum(product[h * HEAD_DIM : (h + 1) * HEAD_DIM], axis=0, keepdims=True) for h in range(2)
+    ]
+
+    def body(use_mask, block, carry):
+        span = key_span(info, block)
+        keys = key_ref[span, :]
+        values = value_ref[span, :]
+        probs, slopes, out = [], [], []
+        for h in range(2):
+            scores = dot(keys, queries[h], NT)
+            if use_mask:
+                scores = masked(scores, bounds_ref, block)
+            prob = jnp.exp(scores - lse[h : h + 1, :])
+            prob_grad = dot(values, grads[h], NT)
+            slope = (prob * (prob_grad - deltas[h])).astype(jnp.bfloat16)
+            probs.append(prob.astype(jnp.bfloat16))
+            slopes.append(slope)
+            out.append(carry[h] + dot(turned[h * HEAD_DIM : (h + 1) * HEAD_DIM, span], slope))
+        value_total[span, :] += dot(jnp.concatenate(probs, axis=1), grad_stack)
+        key_total[span, :] += dot(jnp.concatenate(slopes, axis=1), query_stack)
+        return tuple(out)
+
+    zero = jnp.zeros((HEAD_DIM, 256), jnp.float32)
+    heads = three_loops(info, step, body, (zero, zero))
+    rows = (jnp.concatenate(heads, axis=0).T * HEAD_DIM ** (-0.5)).astype(jnp.bfloat16)
+    query_grad[...] = rows
+    query_sum[0:1, :] += jnp.sum(rows.astype(jnp.float32), axis=0, keepdims=True)
+
+    @pl.when(step == pl.num_programs(1) - 1)
+    def _():
+        key_grad[...] = key_total[...].astype(jnp.bfloat16)
+        rounded = value_total[...].astype(jnp.bfloat16)
+        value_grad[...] = rounded
+        value_sum[...] = jnp.zeros_like(value_sum)
+        value_sum[0:1, :] = jnp.sum(rounded.astype(jnp.float32), axis=0, keepdims=True)
+
+
+def attend_back(info, queries, keys, values, bounds, contexts, grads, lses):
+    rows = jax.ShapeDtypeStruct((2048, 512), jnp.bfloat16)
+    sums = jax.ShapeDtypeStruct((8, 512), jnp.float32)
+    own = pl.BlockSpec((256, 128), lambda p, i, s: (jnp.minimum(i, 3), p))
+    other = pl.BlockSpec((256, 128), lambda p, i, s: (jnp.maximum(i - 4, 0), p))
+    column = pl.BlockSpec((2048, 128), lambda p, i, s: (0, p))
+    sum_spec = pl.BlockSpec((8, 128), lambda p, i, s: (0, p))
+    return pl.pallas_call(
+        attend_back_kernel,
+        out_shape=(rows, rows, rows, sums, sums),
+        grid_spec=pltpu.PrefetchScalarGridSpec(
+            num_scalar_prefetch=1,
+            grid=(4, 8),
+            in_specs=[
+                pl.BlockSpec((256, 128), lambda p, i, s: (i, p)),
+                column,
+                column,
+                pl.BlockSpec((8, 256), lambda p, i, s: (0, i)),
+                own,
+                other,
+                own,
+                other,
+                pl.BlockSpec((1, 8, 256), lambda p, i, s: (p, 0, jnp.minimum(i, 3))),
+                pl.BlockSpec((1, 8, 256), lambda p, i, s: (p, 0, jnp.maximum(i - 4, 0))),
+            ],
+            out_specs=[
+                pl.BlockSpec((256, 128), lambda p, i, s: (i, p)),
+                column,
+                column,
+                sum_spec,
+                sum_spec,
+            ],
+            scratch_shapes=[
+                pltpu.VMEM((128, 2048), jnp.bfloat16),
+                pltpu.VMEM((2048, 128), jnp.float32),
+                pltpu.VMEM((2048, 128), jnp.float32),
+            ],
+        ),
+        compiler_params=params(),
+        name="attend_back",
+    )(info, queries, keys, values, bounds, *contexts, *grads, *lses)
+
+
+def normed(values):
+    average = jnp.mean(values, axis=-1, keepdims=True)
+    centred = values - average
+    inverse = lax.rsqrt(jnp.mean(centred * centred, axis=-1, keepdims=True) + EPSILON)
+    return (centred * inverse, inverse)
+
+
+def normed_back(upstream, unit, inverse, gain):
+    scaled = upstream * gain
+    inner_mean = jnp.mean(scaled, axis=-1, keepdims=True)
+    cross_mean = jnp.mean(scaled * unit, axis=-1, keepdims=True)
+    return inverse * (scaled - inner_mean - unit * cross_mean)
+
+
+def column_total(values):
+    return jnp.sum(values, axis=0, keepdims=True)
+
+
+def middle_kernel(info, *refs):
+    up_pieces, down_pieces = refs[:8], refs[8:16]
+    own_ref, other_ref, token_ref, upstream_ref, vector_ref, up_bias_ref = refs[16:22]
+    (
+        layer_ref, hidden_ref, act_ref, mixed_ref, up_grad_ref, attended_ref, first_ref,
+        grad_own_ref, grad_other_ref, sums_ref, up_sum_ref,
+    ) = refs[22:33]
+    up_weight, down_weight, out_weight, slope_ref, sems = refs[33:]
+    f, t, core = info[0], info[1], info[2]
+    step = pl.program_id(0)
+
+    @pl.when(step == 0)
+    def _():
+        out_copies, up_copies, down_copies = [], [], []
+        for offset in range(8):
+            columns = pl.ds(pl.multiple_of((f ^ offset) * 128, 128), 128)
+            for place in range(4):
+                slice_of = t ^ STEPS[place]
+                row = ((slice_of // 2) ^ core) * 512 + (slice_of % 2) * 256
+                out_copies.append(
+                    pltpu.make_async_copy(
+                        down_pieces[offset].at[place, pl.ds(1024, 256), :],
+                        out_weight.at[pl.ds(pl.multiple_of(row, 256), 256), columns],
+                        sems.at[16 + offset * 4 + place],
+                    )
+                )
+            up_copies.append(
+                pltpu.make_async_copy(up_pieces[offset], up_weight.at[:, columns, :], sems.at[offset])
+            )
+            down_copies.append(
+                pltpu.make_async_copy(
+                    down_pieces[offset].at[:, pl.ds(0, 1024), :],
+                    down_weight.at[:, :, columns],
+                    sems.at[8 + offset],
+                )
+            )
+        copies = out_copies + up_copies + down_copies
+        for copy in copies:
+            copy.start()
+        for copy in copies:
+            copy.wait()
+        sums_ref[...] = jnp.zeros_like(sums_ref)
+        up_sum_ref[...] = jnp.zeros_like(up_sum_ref)
+
+    vectors = [vector_ref[k : k + 1, :] for k in range(6)]
+    out_bias, gain_one, shift_one, down_bias, gain_two, shift_two = vectors
+    attended = dot(own_ref[...], out_weight[0:512, :]) + dot(other_ref[...], out_weight[512:1024, :])
+    unit_one, inverse_one = normed(token_ref[...].astype(jnp.float32) + attended + out_bias)
+    hidden = (unit_one * gain_one + shift_one).astype(jnp.bfloat16)
+    hidden_ref[...] = hidden
+    mixed = jnp.zeros(unit_one.shape, jnp.float32)
+    for place in range(4):
+        span = pl.ds(place * 1024, 1024)
+        pre = dot(hidden, up_weight[place]) + up_bias_ref[place : place + 1, :]
+        square = pre * pre
+        bend = jnp.tanh(0.7978845608028654 * pre * (1.0 + 0.044715 * square))
+        half = 0.5 * (1.0 + bend)
+        act = (pre * half).astype(jnp.bfloat16)
+        act_ref[:, span] = act
+        slope_ref[:, span] = half + 0.5 * pre * (1.0 - bend * bend) * (
+            0.7978845608028654 * (1.0 + 0.134145 * square)
+        )
+        mixed = mixed + dot(act, down_weight[place])
+    unit_two, inverse_two = normed(hidden.astype(jnp.float32) + mixed + down_bias)
+    layer_ref[...] = (unit_two * gain_two + shift_two).astype(jnp.bfloat16)
+    upstream = upstream_ref[...].astype(jnp.float32)
+    second = normed_back(upstream, unit_two, inverse_two, gain_two)
+    sums_ref[3:4, :] += column_total(second)
+    sums_ref[4:5, :] += column_total(upstream * unit_two)
+    sums_ref[5:6, :] += column_total(upstream)
+    mixed_grad = second.astype(jnp.bfloat16)
+    mixed_ref[...] = mixed_grad
+    back = second
+    for place in range(4):
+        span = pl.ds(place * 1024, 1024)
+        up_grad = (dot(mixed_grad, down_weight[place], NT) * slope_ref[:, span]).astype(jnp.bfloat16)
+        up_grad_ref[:, span] = up_grad
+        up_sum_ref[place : place + 1, :] += column_total(up_grad.astype(jnp.float32))
+        back = back + dot(up_grad, up_weight[place], NT)
+    first = normed_back(back, unit_one, inverse_one, gain_one)
+    sums_ref[0:1, :] += column_total(first)
+    sums_ref[1:2, :] += column_total(back * unit_one)
+    sums_ref[2:3, :] += column_total(back)
+    first_ref[...] = first
+    rounded = first.astype(jnp.bfloat16)
+    attended_ref[...] = rounded
+    grad_own_ref[...] = dot(rounded, out_weight[0:512, :], NT).astype(jnp.bfloat16)
+    grad_other_ref[...] = dot(rounded, out_weight[512:1024, :], NT).astype(jnp.bfloat16)
+
+
+def middle(info, up_pieces, down_pieces, own, other, tokens, upstream, vectors, up_bias):
+    tile = 256
+
+    def rows(width):
+        return pl.BlockSpec((tile, width), lambda i, s: (i, 0))
+
+    def fixed(shape):
+        return pl.BlockSpec(shape, lambda i, s: (0, 0))
+
+    def array(width, kind=jnp.bfloat16):
+        return jax.ShapeDtypeStruct((1024, width), kind)
+
+    return pl.pallas_call(
+        middle_kernel,
+        out_shape=(
+            array(1024), array(1024), array(4096), array(1024), array(4096), array(1024),
+            array(1024, jnp.float32), array(512), array(512),
+            jax.ShapeDtypeStruct((8, 1024), jnp.float32),
+            jax.ShapeDtypeStruct((8, 1024), jnp.float32),
+        ),
+        grid_spec=pltpu.PrefetchScalarGridSpec(
+            num_scalar_prefetch=1,
+            grid=(4,),
+            in_specs=[ANY] * 16
+            + [rows(512), rows(512), rows(1024), rows(1024), fixed((8, 1024)), fixed((8, 1024))],
+            out_specs=[
+                rows(1024), rows(1024), rows(4096), rows(1024), rows(4096), rows(1024),
+                rows(1024), rows(512), rows(512), fixed((8, 1024)), fixed((8, 1024)),
+            ],
+            scratch_shapes=[
+                pltpu.VMEM((4, 1024, 1024), jnp.bfloat16),
+                pltpu.VMEM((4, 1024, 1024), jnp.bfloat16),
+                pltpu.VMEM((1024, 1024), jnp.bfloat16),
+                pltpu.VMEM((tile, 4096), jnp.float32),
+                pltpu.SemaphoreType.DMA((48,)),
+            ],
+        ),
+        compiler_params=params(),
+        name="middle",
+    )(info, *up_pieces, *down_pieces, own, other, tokens, upstream, vectors, up_bias)
+
+
+def turn_columns(turned, refs):
+    for k in range(4):
+        turned[k * 128 : (k + 1) * 128, :] = refs[k][...].T
+
+
+def wide_grad_kernel(has_other, info, *refs):
+    left, right = refs[:4], refs[4]
+    others = refs[5:7] if has_other else None
+    keep_ref, send_ref, turned = refs[-3:]
+
+    @pl.when(pl.program_id(0) == 0)
+    def _():
+        turn_columns(turned, left)
+
+    result = dot(turned[...], right[...])
+    for k in range(4):
+        part = result[k * 128 : (k + 1) * 128]
+        target = keep_ref if k < 2 else send_ref
+        if has_other:
+            part = part + others[k // 2][k % 2, 0].astype(jnp.float32)
+        target[k % 2, 0] = part.astype(jnp.bfloat16)
+
+
+def left_specs(rows, order, core_bit):
+    return [
+        pl.BlockSpec((rows, 128), lambda n, s, o=offset: (0, s[0] ^ (o | core_bit))) for offset in order
+    ]
+
+
+def wide_grad(info, left, right, order, core_bit, others=None):
+    shape = jax.ShapeDtypeStruct((2, 4, 128, 1024), jnp.bfloat16)
+    part = pl.BlockSpec((2, 1, 128, 512), lambda n, s: (0, n // 2, 0, n % 2))
+    return pl.pallas_call(
+        partial(wide_grad_kernel, others is not None),
+        out_shape=(shape, shape),
+        grid_spec=pltpu.PrefetchScalarGridSpec(
+            num_scalar_prefetch=1,
+            grid=(8,),
+            in_specs=left_specs(1024, order, core_bit)
+            + [pl.BlockSpec((1024, 512), lambda n, s: (0, n))]
+            + ([part, part] if others is not None else []),
+            out_specs=[part, part],
+            scratch_shapes=[pltpu.VMEM((512, 1024), jnp.bfloat16)],
+        ),
+        compiler_params=params(),
+        name="wide_grad",
+    )(info, left, left, left, left, right, *(others or ()))
+
+
+def out_grad_kernel(has_other, info, *refs):
+    left, own, other = refs[:4], refs[4], refs[5]
+    others = refs[6:8] if has_other else None
+    keep_ref, send_ref, turned = refs[-3:]
+    step = pl.program_id(0)
+
+    @pl.when(step == 0)
+    def _():
+        turn_columns(turned, left)
+
+    result = dot(turned[...], jnp.where(step < 2, own[...], other[...]))
+    for k in range(4):
+        part = result[k * 128 : (k + 1) * 128]
+        target = keep_ref if k < 2 else send_ref
+        if has_other:
+            part = part + others[k // 2][k % 2, 0].astype(jnp.float32)
+        target[k % 2, 0] = part.astype(jnp.bfloat16)
+
+
+def out_grad_parts(info, left, own, other, order, core_bit, others=None):
+    shape = jax.ShapeDtypeStruct((2, 4, 128, 256), jnp.bfloat16)
+
+    def place(n, s):
+        return place_of(s[1] ^ (2 * ((n // 2) ^ s[2]) + n % 2))
+
+    part = pl.BlockSpec((2, 1, 128, 256), lambda n, s: (0, place(n, s), 0, 0))
+    return pl.pallas_call(
+        partial(out_grad_kernel, others is not None),
+        out_shape=(shape, shape),
+        grid_spec=pltpu.PrefetchScalarGridSpec(
+            num_scalar_prefetch=1,
+            grid=(4,),
+            in_specs=left_specs(1024, order, core_bit)
+            + [
+                pl.BlockSpec((1024, 256), lambda n, s: (0, jnp.minimum(n, 1))),
+                pl.BlockSpec((1024, 256), lambda n, s: (0, jnp.maximum(n - 2, 0))),
+            ]
+            + ([part, part] if others is not None else []),
+            out_specs=[part, part],
+            scratch_shapes=[pltpu.VMEM((512, 1024), jnp.bfloat16)],
+        ),
+        compiler_params=params(),
+        name="out_grad",
+    )(info, left, left, left, left, own, other, *(others or ()))
+
+
+def qkv_grad_kernel(info, *refs):
+    left, rights = refs[:4], refs[4:7]
+    keep_ref, send_ref, turned = refs[-3:]
+
+    @pl.when(pl.program_id(0) == 0)
+    def _():
+        turn_columns(turned, left)
+
+    for which in range(3):
+        result = dot(turned[...], rights[which][...])
+        for k in range(4):
+            target = keep_ref if k < 2 else send_ref
+            target[k % 2, 0, which] = result[k * 128 : (k + 1) * 128].astype(jnp.bfloat16)
+
+
+def qkv_grad(info, left, rights, order, core_bit):
+    shape = jax.ShapeDtypeStruct((2, 2, 3, 128, 256), jnp.bfloat16)
+    part = pl.BlockSpec((2, 1, 3, 128, 256), lambda n, s: (0, n, 0, 0, 0))
+    return pl.pallas_call(
+        qkv_grad_kernel,
+        out_shape=(shape, shape),
+        grid_spec=pltpu.PrefetchScalarGridSpec(
+            num_scalar_prefetch=1,
+            grid=(2,),
+            in_specs=left_specs(2048, order, core_bit)
+            + [pl.BlockSpec((2048, 256), lambda n, s: (0, n))] * 3,
+            out_specs=[part, part],
+            scratch_shapes=[pltpu.VMEM((512, 2048), jnp.bfloat16)],
+        ),
+        compiler_params=params(),
+        name="qkv_grad",
+    )(info, left, left, left, left, *rights)
+
+
+def token_grad_kernel(has_other, info, *refs):
+    grads, weight = refs[:3], refs[3]
+    total = dot(grads[0][...], weight[0], NT)
+    total = total + dot(grads[1][...], weight[1], NT)
+    total = total + dot(grads[2][...], weight[2], NT)
+    if has_other:
+        total = total + refs[4][...].astype(jnp.float32) + refs[5][...]
+    refs[-1][...] = total.astype(jnp.bfloat16)
+
+
+def token_grad(info, grads, weight, half, other=None, first=None):
+    extra = [] if other is None else [other, first]
+    return pl.pallas_call(
+        partial(token_grad_kernel, other is not None),
+        out_shape=jax.ShapeDtypeStruct((1024, 1024), jnp.bfloat16),
+        grid_spec=pltpu.PrefetchScalarGridSpec(
+            num_scalar_prefetch=1,
+            grid=(4,),
+            in_specs=[pl.BlockSpec((256, 512), lambda i, s: (half * 4 + i, 0))] * 3
+            + [pl.BlockSpec((3, 1024, 512), lambda i, s: (0, 0, 0))]
+            + [pl.BlockSpec((256, 1024), lambda i, s: (i, 0))] * len(extra),
+            out_specs=pl.BlockSpec((256, 1024), lambda i, s: (i, 0)),
+        ),
+        compiler_params=params(),
+        name="token_grad",
+    )(info, *grads, weight, *extra)
+
+
+def low(values):
+    return values.astype(jnp.bfloat16)
+
+
+def wide(values):
+    return values.astype(jnp.float32)
+
+
+def plane_sums(keep, send, first_bits, second_bits):
+    came = swap(send, first_bits, 0)
+    passed = swap(low(wide(keep[1]) + wide(came[1])), second_bits, 0)
+    return wide(keep[0]) + wide(came[0]) + wide(passed)
+
+
+def column_sums(total):
+    came = swap(low(total[2:4]), 0, 1)
+    total = total[0:2] + wide(came)
+    return total[0] + wide(swap(low(total[1]), 0, 2))
+
+
+def chip_shards(
+    inputs,
+    w_query,
+    w_key,
+    w_value,
+    b_query,
+    b_value,
+    w_output,
+    b_output,
+    attn_gain,
+    attn_shift,
+    w_up,
+    b_up,
+    w_down,
+    b_down,
+    mlp_gain,
+    mlp_shift,
+    doc_lengths,
+    out_grad,
+):
+    f, t = lax.axis_index("fsdp"), lax.axis_index("tp")
+    core, micro = f % 2, t // 2
+
+    narrow = jnp.concatenate(
+        [
+            jnp.concatenate([b_up[0], b_query[0], b_value[0], jnp.zeros((64,), jnp.bfloat16)])[None],
+            jnp.concatenate(
+                [b_output, attn_gain, attn_shift, b_down, mlp_gain, mlp_shift, jnp.zeros((64,), jnp.bfloat16)]
+            )[None],
+            jnp.zeros((14, 256), jnp.bfloat16),
+        ]
+    )
+    qkv_pieces = gather_pieces(jnp.concatenate([w_query, w_key, w_value, narrow]), 2, 4)
+    token_a, token_b = to_sequences(inputs, t)
+    up_pieces = gather_pieces(w_up, 2, 4)
+    down_pieces = gather_pieces(jnp.concatenate([w_down, w_output]), 4, 2)
+    upstream_a, upstream_b = to_sequences(out_grad, t)
+    other_a, other_b = swap(token_a, 1, 0), swap(token_b, 1, 0)
+    lengths = jnp.where(t % 2 == core, doc_lengths, swap(doc_lengths, 1, 0))[micro, 0]
+
+    narrow_rows = jnp.stack([piece[:, 384:386] for piece in qkv_pieces]).reshape(32, 2, 256)
+    f_ids, t_ids = jnp.arange(8), jnp.arange(4)
+    order = ((f_ids ^ f)[:, None] * 4 + place_of(t_ids ^ t)[None, :]).reshape(-1)
+    narrow_rows = wide(jnp.take(narrow_rows, order, axis=0)).reshape(8, 4, 2, 256)
+    vectors = narrow_rows[:, :, 1, :192].reshape(32, 6, 32).transpose(1, 0, 2).reshape(6, 1024)
+    vectors = jnp.pad(vectors, ((0, 2), (0, 0)))
+    quad = t ^ jnp.array(STEPS)
+    up_bias = narrow_rows[:, :, 0, :128].transpose(1, 0, 2).reshape(4, 1024)
+    up_bias = jnp.pad(jnp.take(up_bias, quad, axis=0), ((0, 4), (0, 0)))
+    head_bias = narrow_rows[:, :, 0, 128:192].reshape(8, 4, 2, 32).transpose(2, 1, 0, 3).reshape(2, 2, 512)
+    head_bias = lax.dynamic_index_in_dim(head_bias, core, 1, keepdims=False)
+    head_bias = jnp.pad(head_bias, ((0, 6), (0, 0)))
+
+    ends = jnp.cumsum(lengths)
+    places = jnp.arange(2048, dtype=jnp.int32)
+    places = places ^ (core * 1024)
+    past = ends[None, :] <= places[:, None]
+    doc_start = jnp.max(jnp.where(past, ends[None, :], 0), axis=1)
+    doc_end = jnp.min(jnp.where(past, 2048, ends[None, :]), axis=1)
+    low_bound = jnp.maximum(doc_start, places - (WINDOW - 1))
+    high_bound = jnp.minimum(doc_end, places + WINDOW)
+    bounds = jnp.concatenate([low_bound[None], high_bound[None], jnp.zeros((6, 2048), jnp.int32)])
+    low_blocks, high_blocks = low_bound.reshape(8, 256), high_bound.reshape(8, 256)
+    block_lo = jnp.min(low_blocks, axis=1) // 256
+    block_hi = (jnp.max(high_blocks, axis=1) + 255) // 256
+    full_lo = (jnp.max(low_blocks, axis=1) + 255) // 256
+    full_hi = jnp.min(high_blocks, axis=1) // 256
+    none = full_lo >= full_hi
+    full_lo, full_hi = jnp.where(none, block_hi, full_lo), jnp.where(none, block_hi, full_hi)
+    table = jnp.stack([block_lo, block_hi, full_lo, full_hi], axis=1).reshape(-1)
+    info = jnp.concatenate(
+        [jnp.stack([f, t, core, micro, core * 0, core * 0, core * 0, core * 0]), table]
+    ).astype(jnp.int32)
+
+    tokens, weight, queries, keys, values = project(
+        info, qkv_pieces, (token_a, token_b, other_a, other_b), head_bias
+    )
+    context_sent, lse_other = attend(info, queries, keys, values, bounds, 1)
+    context_came = swap(context_sent, 1, 0)
+    context_own, lse_own = attend(info, queries, keys, values, bounds, 0)
+    upstream = jnp.where(
+        micro == 0,
+        jnp.concatenate([upstream_a, upstream_b]),
+        jnp.concatenate([upstream_b, upstream_a]),
+    )
+    (
+        layer_rows, hidden, act, mixed_grad, up_grad, attended, first,
+        grad_own, grad_sent, vector_sums, up_sums,
+    ) = middle(info, up_pieces, down_pieces, context_own, context_came, tokens, upstream, vectors, up_bias)
+    grad_came = swap(grad_sent, 1, 0)
+    layer_out = to_homes(layer_rows, t)
+
+    up_order, down_order = (0, 4, 2, 6), (0, 2, 4, 6)
+    down_sent = wide_grad(info, mixed_grad, act, down_order, 1)
+    up_sent = wide_grad(info, hidden, up_grad, up_order, 1)
+    out_sent = out_grad_parts(info, attended, context_own, context_came, down_order, 1)
+    down_came = tuple(swap(part, 1, 0) for part in down_sent)
+    up_came = tuple(swap(part, 1, 0) for part in up_sent)
+    out_came = tuple(swap(part, 1, 0) for part in out_sent)
+    down_parts = wide_grad(info, mixed_grad, act, down_order, 0, down_came)
+    up_parts = wide_grad(info, hidden, up_grad, up_order, 0, up_came)
+    out_parts = out_grad_parts(info, attended, context_own, context_came, down_order, 0, out_came)
+    grad_down = column_sums(plane_sums(*down_parts, 4, 2)).T
+    grad_up = column_sums(plane_sums(*up_parts, 2, 4))
+    grad_output = column_sums(plane_sums(*out_parts, 4, 2)).T
+
+    by_tp = jnp.take(up_sums[:4], place_of(t_ids ^ t), axis=0)
+    sums = jnp.concatenate(
+        [
+            vector_sums[:6].reshape(6, 32, 32).transpose(1, 0, 2).reshape(32, 192),
+            by_tp.reshape(4, 8, 128).transpose(1, 0, 2).reshape(32, 128),
+        ],
+        axis=1,
+    )
+    sums = lax.psum_scatter(sums, AXES, scatter_dimension=0, tiled=True)[0]
+
+    query_grad, key_grad, value_grad, query_sum, value_sum = attend_back(
+        info, queries, keys, values, bounds,
+        (context_own, context_sent), (grad_own, grad_came), (lse_own, lse_other),
+    )
+    grads = (query_grad, key_grad, value_grad)
+    token_sent = token_grad(info, grads, weight, 1)
+    token_came = swap(token_sent, 1, 0)
+    qkv_sent = qkv_grad(info, tokens, grads, up_order, 1)
+    qkv_came = tuple(swap(part, 1, 0) for part in qkv_sent)
+    token_rows = token_grad(info, grads, weight, 0, token_came, first)
+    input_grad = to_homes(token_rows, t)
+    qkv_own = plane_sums(*qkv_grad(info, tokens, grads, up_order, 0), 2, 4)
+    qkv_other = plane_sums(*qkv_came, 2, 4)
+    by_slice = jnp.where(
+        core == 0,
+        jnp.concatenate([qkv_own, qkv_other]),
+        jnp.concatenate([qkv_other, qkv_own]),
+    )
+    qkv_total = column_sums(jnp.take(by_slice, quad, axis=0))
+
+    head_sums = jnp.stack([query_sum[0], value_sum[0]])
+    head_sums = jnp.where(
+        core == 0,
+        jnp.concatenate([head_sums, jnp.zeros_like(head_sums)], axis=1),
+        jnp.concatenate([jnp.zeros_like(head_sums), head_sums], axis=1),
+    )
+    head_sums = head_sums.reshape(2, 4, 8, 32).transpose(2, 1, 0, 3).reshape(32, 64)
+    head_sums = lax.psum_scatter(head_sums, AXES, scatter_dimension=0, tiled=True)[0]
+    return (
+        layer_out,
+        input_grad,
+        qkv_total[0],
+        qkv_total[1],
+        qkv_total[2],
+        head_sums[None, :32],
+        head_sums[None, 32:],
+        grad_output,
+        sums[0:32],
+        sums[32:64],
+        sums[64:96],
+        grad_up,
+        sums[None, 192:320],
+        grad_down,
+        sums[96:128],
+        sums[128:160],
+        sums[160:192],
+    )
+
+
 def solution(mesh):
     in_specs = (
         P(None, ("fsdp", "tp"), None),
@@ -406,4 +1236,5 @@
         P(("fsdp", "tp")),
         P(("fsdp", "tp")),
     )
-    return jax.shard_map(shards, mesh=mesh, in_specs=in_specs, out_specs=out_specs, check_vma=False)
+    body = chip_shards if (mesh.shape["fsdp"], mesh.shape["tp"]) == (8, 4) else shards
+    return jax.shard_map(body, mesh=mesh, in_specs=in_specs, out_specs=out_specs, check_vma=False)

time: 1900 us -> 995 us (0.52)
  waiting for transfers between devices: 949 us -> 302 us
  matrix products: 500 us -> 0 us
  Pallas kernels: 0 us -> 484 us
  other arithmetic: 226 us -> 37.1 us
  blocking collectives: 134 us -> 38.3 us
  starting transfers between devices: 2.02 us -> 88.8 us
  local copies, waits for them, and re-layouts: 61.2 us -> 38.4 us
    dot_general x84 -> x0, matrix products: 500 us -> none  [the longest x8 85 us: attention_backward(): jnp.einsum('qhd,khd->hqk', grad_heads, value_heads, preferred_element_typ...]
    pallas_call x0 -> x15, Pallas kernels: none -> 484 us  [the longest x1 157 us: attend_back(): pl.pallas_call(attend_back_kernel, out_shape=(rows, rows, rows, sums, sum...]
    all_gather x10 -> x0, waiting for transfers between devices: 436 us -> none  [the longest x2 148 us: shards(): lax.all_gather(second_grad.astype(jnp.bfloat16), 'tp', axis=0, tiled=True)]
    reduce_scatter x8 -> x0, waiting for transfers between devices: 430 us -> none  [the longest x2 145 us: shards(): lax.psum_scatter(jnp.einsum('sf,df->sd', up_grad, up_full, preferred_elem...]
    ppermute x0 -> x67, waiting for transfers between devices: none -> 302 us  [the longest x59 285 us: swap(): return lax.ppermute(values, AXES, pairs)]
    all_gather x6 -> x0, blocking collectives: 119 us -> none  [the longest x1 69.6 us: shards(): lax.all_gather(jnp.stack([b_output, attn_gain, attn_shift, b_down, mlp_ga...]
    convert_element_type x15 -> x6, other arithmetic: 112 us -> 8.83 us  [the longest x5 8.74 us: low(): return values.astype(jnp.bfloat16)]
    reduce_sum x21 -> x0, other arithmetic: 90.7 us -> none  [the longest x8 65.6 us: attention_forward(): row_total = jnp.sum(exponent, axis=-1, keepdims=True)]
  transfers between devices with their start and end apart: 20 -> 67, of which waited for: 16 -> 18; matrix products, arithmetic and copies ran while one was open for 32% -> 6% of each run, Pallas kernels for 0% -> 43%
where the time goes in v1:
time: 995 us; the launch traced here: 990 us
  Pallas kernels  484 us (49%)
  waiting for transfers between devices  302 us (30%)
  starting transfers between devices  88.8 us (9%)
  local copies, waits for them, and re-layouts  38.4 us (4%)
  blocking collectives  38.3 us (4%)
  other arithmetic  37.1 us (4%)
    ppermute x59, waiting for transfers between devices, swap(): return lax.ppermute(values, AXES, pairs)  285 us
    pallas_call x1, Pallas kernels, attend_back(): pl.pallas_call(attend_back_kernel, out_shape=(rows, rows, rows, sums, sum...  157 us
    pallas_call x2, Pallas kernels, attend(): pl.pallas_call(partial(attend_kernel, first_block), out_shape=(jax.ShapeD...  156 us
    ppermute x59, starting transfers between devices, swap(): return lax.ppermute(values, AXES, pairs)  70.7 us
    pallas_call x1, Pallas kernels, middle(): pl.pallas_call(middle_kernel, out_shape=(array(1024), array(1024), array(...  61.1 us
    pallas_call x4, Pallas kernels, wide_grad(): pl.pallas_call(partial(wide_grad_kernel, others is not None), out_shape=(...  47.9 us
    unnamed x1, blocking collectives  38.3 us
  transfers between devices with their start and end apart: 67, of which 18 were waited for; matrix products, arithmetic and copies ran while one was open for 6% of the time, Pallas kernels for 43%

profile of v1, /device:TPU:0, one launch (start us, length us, event | category | flops | bytes accessed | tf_op | source)
XLA Modules:
  0.0 989.9 jit_solution(207853041472367892)
XLA Ops:
  1.4 4.1 concatenate.56
  5.5 2.7 concatenate.57
  8.2 4.1 collective-permute-start.19
  14.3 2.9 collective-permute-start.1
  17.2 3.1 dynamic-slice_bitcast_fusion.6
  20.3 9.6 collective-permute-start.28
  29.9 9.5 collective-permute-done.19
  40.2 30.4 %collective-permute-done.1 = bf16[128,1024]{1,0:T(8,128)(2,1)} collective-permute-done((bf16[128,1024]{1,0:T(8,128)(2,1)}, bf16[128,1024]{1,0:T(8,128)(2,1)}, u32[]{:S(2)}, u32[]{:S(2)}) %collective-permute-start.1) | collective-permute-done | bytes 262176 | tf_op jit(solution)/shard_map/ppermute | solution.py:398
  70.6 1.8 pad_maximum_fusion.4
  72.4 2.0 collective-permute-start.2
  77.0 15.5 %collective-permute-done.20 = bf16[2,400,256]{2,1,0:T(8,128)(2,1)} collective-permute-done((bf16[2,400,256]{2,1,0:T(8,128)(2,1)}, bf16[2,400,256]{2,1,0:T(8,128)(2,1)}, u32[]{:S(2)}, u32[]{:S(2)}) %collective-permute-start.20) | collective-permute-done | bytes 409632 | tf_op jit(solution)/shard_map/ppermute | solution.py:398
  92.5 1.9 collective-permute-start.33
  94.4 17.0 %collective-permute-done.2 = bf16[2,128,1024]{2,1,0:T(8,128)(2,1)} collective-permute-done((bf16[2,128,1024]{2,1,0:T(8,128)(2,1)}, bf16[2,128,1024]{2,1,0:T(8,128)(2,1)}, u32[]{:S(2)}, u32[]{:S(2)}) %collective-permute-start.2) | collective-permute-done | bytes 524320 | tf_op jit(solution)/shard_map/ppermute | solution.py:398
  112.7 15.1 %collective-permute-done.11 = bf16[2,1280,128]{2,1,0:T(8,128)(2,1)} collective-permute-done((bf16[2,1280,128]{2,1,0:T(8,128)(2,1)}, bf16[2,1280,128]{2,1,0:T(8,128)(2,1)}, u32[]{:S(2)}, u32[]{:S(2)}) %collective-permute-start.11) | collective-permute-done | bytes 655392 | tf_op jit(solution)/shard_map/ppermute | solution.py:398
  132.9 17.3 %collective-permute-done.34 = bf16[512,1024]{1,0:T(8,128)(2,1)} collective-permute-done((bf16[512,1024]{1,0:T(8,128)(2,1)}, bf16[512,1024]{1,0:T(8,128)(2,1)}, u32[]{:S(2)}, u32[]{:S(2)}) %collective-permute-start.34) | collective-permute-done | bytes 1048608 | tf_op jit(solution)/shard_map/ppermute | solution.py:415
  154.3 16.7 %collective-permute-done.4.refs_2_ = bf16[4,128,1024]{2,1,0:T(8,128)(2,1)} collective-permute-done((bf16[4,128,1024]{2,1,0:T(8,128)(2,1)S(1)}, bf16[4,128,1024]{2,1,0:T(8,128)(2,1)}, u32[]{:S(2)}, u32[]{:S(2)}) %collective-permute-start.4) | collective-permute-done | bytes 1048608 | tf_op jit(solution)/shard_map/ppermute | solution.py:398
  176.9 42.1 %collective-permute-done.26.refs_6_ = bf16[4,400,256]{2,1,0:T(8,128)(2,1)} collective-permute-done((bf16[4,400,256]{2,1,0:T(8,128)(2,1)}, bf16[4,400,256]{2,1,0:T(8,128)(2,1)}, u32[]{:S(2)}, u32[]{:S(2)}) %collective-permute-start.26) | collective-permute-done | bytes 819232 | tf_op jit(solution)/shard_map/ppermute | solution.py:398
  228.5 19.3 %collective-permute-done.8.refs_6_ = bf16[4,128,1024]{2,1,0:T(8,128)(2,1)} collective-permute-done((bf16[4,128,1024]{2,1,0:T(8,128)(2,1)}, bf16[4,128,1024]{2,1,0:T(8,128)(2,1)}, u32[]{:S(2)}, u32[]{:S(2)}) %collective-permute-start.8) | collective-permute-done | bytes 1048608 | tf_op jit(solution)/shard_map/ppermute | solution.py:398
  247.8 3.6 collective-permute-done.17.refs_14_
  252.4 13.9 %qkv.1 = (bf16[2048,1024]{1,0:T(8,128)(2,1)}, bf16[3,1024,512]{2,1,0:T(8,128)(2,1)}, bf16[2048,512]{1,0:T(8,128)(2,1)}, bf16[2048,512]{1,0:T(8,128)(2,1)}, bf16[2048,512]{1,0:T(8,128)(2,1)}) custom-call(s32[40]{0:T(128)} %concatenate.51.info, bf16[4,400,256]{2,1,0:T(8,128)(2,1)} %copy-done.3, bf16[4,400,256]{2,1,0:T(8,128)(2,1)} %collective-permute-done.21.refs_1_, ...), custom_call_target="tpu_custom_call" | custom-call | tf_op jit(solution)/shard_map/qkv/pallas_call | solution.py:484
  266.3 78.2 %attend.3 = (bf16[1024,512]{1,0:T(8,128)(2,1)}, f32[4,8,1024]{2,1,0:T(8,128)}) custom-call(s32[40]{0:T(128)} %concatenate.51.info, bf16[2048,512]{1,0:T(8,128)(2,1)} %get-tuple-element.59.query_ref, bf16[2048,512]{1,0:T(8,128)(2,1)} %get-tuple-element.60.key_ref, bf16[2048,512]{1,0:T(8,128)(2,1)} %get-tuple-element.61.value_ref, ...), custom_call_target="tpu_custom_call" | custom-call | tf_op jit(solution)/shard_map/attend/pallas_call | solution.py:576
  344.6 12.1 %collective-permute-start.9 = (bf16[4,128,1024]{2,1,0:T(8,128)(2,1)}, bf16[4,128,1024]{2,1,0:T(8,128)(2,1)S(1)}, u32[]{:S(2)}, u32[]{:S(2)}) collective-permute-start(bf16[4,128,1024]{2,1,0:T(8,128)(2,1)} %collective-permute-done.8.refs_6_), channel_id=1, source_target_pairs={{0,4},{1,5},{2,6},{3,7},{4,0},{5,1},{6,2},{7,3},{8,12},{9,13},{10,... | collective-permute-start | bytes 3145736 | tf_op jit(solution)/shard_map/ppermute | solution.py:398
  357.7 3.9 maximum_select_fusion.refs_19_
  361.6 78.0 %attend.2 = (bf16[1024,512]{1,0:T(8,128)(2,1)}, f32[4,8,1024]{2,1,0:T(8,128)}) custom-call(s32[40]{0:T(128)} %concatenate.51.info, bf16[2048,512]{1,0:T(8,128)(2,1)} %get-tuple-element.59.query_ref, bf16[2048,512]{1,0:T(8,128)(2,1)} %get-tuple-element.60.key_ref, bf16[2048,512]{1,0:T(8,128)(2,1)} %get-tuple-element.61.value_ref, ...), custom_call_target="tpu_custom_call" | custom-call | tf_op jit(solution)/shard_map/attend/pallas_call | solution.py:576
  443.0 61.1 %middle.1 = (bf16[1024,1024]{1,0:T(8,128)(2,1)}, bf16[1024,1024]{1,0:T(8,128)(2,1)}, bf16[1024,4096]{1,0:T(8,128)(2,1)}, bf16[1024,1024]{1,0:T(8,128)(2,1)}, bf1...) custom-call(s32[40]{0:T(128)} %concatenate.51.info, ...), custom_call_target="tpu_custom_call" | custom-call | tf_op jit(solution)/shard_map/middle/pallas_call | solution.py:827
  504.2 6.3 out_grad.2
  511.1 11.6 %wide_grad.6 = (bf16[2,4,128,1024]{3,2,1,0:T(8,128)(2,1)}, bf16[2,4,128,1024]{3,2,1,0:T(8,128)(2,1)}) custom-call(s32[40]{0:T(128)} %concatenate.51.info, bf16[1024,1024]{1,0:T(8,128)(2,1)} %get-tuple-element.94.refs_0_.refs_1_.refs_2_.refs_3_, bf16[1024,1024]{1,0:T(8,128)(2,1)} %get-tuple-element.94.refs_0_.refs_1_.refs_2_.refs_3_, ...), custom_call_target="tpu_custom_call" | custom-call | tf_op jit(solution)/shard_map/wide_grad/pallas_call | solution.py:889
  524.7 6.3 out_grad.3
  531.0 3.1 dynamic-slice_bitcast_fusion.3
  534.0 1.9 collective-permute-start.35
  535.9 1.8 collective-permute-start.36
  537.7 157.0 %attend_back.1 = (bf16[2048,512]{1,0:T(8,128)(2,1)}, bf16[2048,512]{1,0:T(8,128)(2,1)}, bf16[2048,512]{1,0:T(8,128)(2,1)}, f32[8,512]{1,0:T(8,128)}, f32[8,512]{1,0:T(8,128)}) custom-call(s32[40]{0:T(128)} %concatenate.51.info, bf16[2048,512]{1,0:T(8,128)(2,1)} %get-tuple-element.59.query_ref, bf16[2048,512]{1,0:T(8,128)(2,1)} %get-tuple-element.60.key_ref, ...), custom_call_target="tpu_custom_call" | custom-call | tf_op jit(solution)/shard_map/attend_back/pallas_call | solution.py:671
  694.7 8.6 qkv_grad.2
  703.4 2.8 collective-permute-start.41
  706.1 8.6 collective-permute-start.62
  714.8 11.6 %wide_grad.4 = (bf16[2,4,128,1024]{3,2,1,0:T(8,128)(2,1)}, bf16[2,4,128,1024]{3,2,1,0:T(8,128)(2,1)}) custom-call(s32[40]{0:T(128)} %concatenate.51.info, bf16[1024,1024]{1,0:T(8,128)(2,1)} %get-tuple-element.88.refs_0_.refs_1_.refs_2_.refs_3_, bf16[1024,1024]{1,0:T(8,128)(2,1)} %get-tuple-element.88.refs_0_.refs_1_.refs_2_.refs_3_, ...), custom_call_target="tpu_custom_call" | custom-call | tf_op jit(solution)/shard_map/wide_grad/pallas_call | solution.py:889
  726.9 8.7 qkv_grad.3
  739.5 8.1 token_grad.2
  747.6 38.3 %all-reduce.7 = (f32[32,64]{1,0:T(8,128)S(1)}, f32[32,320]{1,0:T(8,128)S(1)}) all-reduce(f32[32,64]{1,0:T(8,128)S(1)} %reshape.517, f32[32,320]{1,0:T(8,128)S(1)} %pad_maximum_fusion.6), channel_id=2, replica_groups=mesh['fsdp'=8,'tp'=4] {'fsdp','tp'}, use_global_device_ids=true, to_apply=%region_7.9.clone | all-reduce | flops 12288 | bytes 98304
  787.2 2.3 collective-permute-start.45
  789.5 3.3 maximum_select_fusion.1
  795.1 12.4 %wide_grad.7 = (bf16[2,4,128,1024]{3,2,1,0:T(8,128)(2,1)}, bf16[2,4,128,1024]{3,2,1,0:T(8,128)(2,1)}) custom-call(s32[40]{0:T(128)} %concatenate.51.info, bf16[1024,1024]{1,0:T(8,128)(2,1)} %get-tuple-element.94.refs_0_.refs_1_.refs_2_.refs_3_, bf16[1024,1024]{1,0:T(8,128)(2,1)} %get-tuple-element.94.refs_0_.refs_1_.refs_2_.refs_3_, ...), custom_call_target="tpu_custom_call" | custom-call | tf_op jit(solution)/shard_map/wide_grad/pallas_call | solution.py:889
  811.5 2.0 collective-permute-done.52
  813.5 1.8 collective-permute-start.46
  817.2 2.2 collective-permute-start.53
  819.4 12.3 %wide_grad.5 = (bf16[2,4,128,1024]{3,2,1,0:T(8,128)(2,1)}, bf16[2,4,128,1024]{3,2,1,0:T(8,128)(2,1)}) custom-call(s32[40]{0:T(128)} %concatenate.51.info, bf16[1024,1024]{1,0:T(8,128)(2,1)} %get-tuple-element.88.refs_0_.refs_1_.refs_2_.refs_3_, bf16[1024,1024]{1,0:T(8,128)(2,1)} %get-tuple-element.88.refs_0_.refs_1_.refs_2_.refs_3_, ...), custom_call_target="tpu_custom_call" | custom-call | tf_op jit(solution)/shard_map/wide_grad/pallas_call | solution.py:889
  833.5 38.8 %collective-permute-done.46 = bf16[2,3,128,256]{3,2,1,0:T(8,128)(2,1)S(1)} collective-permute-done((bf16[2,3,128,256]{3,2,1,0:T(8,128)(2,1)S(1)}, bf16[2,3,128,256]{3,2,1,0:T(8,128)(2,1)S(1)}, u32[]{:S(2)}, u32[]{:S(2)}) %collective-permute-start.46) | collective-permute-done | bytes 393248 | tf_op jit(solution)/shard_map/ppermute | solution.py:398
  874.6 2.2 collective-permute-start.47
  877.8 9.2 collective-permute-done.47
  887.1 2.8 fusion.1
  891.9 2.6 fusion
  896.6 9.5 token_grad.3
  906.1 1.7 dynamic-slice_bitcast_fusion.1
  908.5 2.2 collective-permute-start.40
  910.8 3.3 collective-permute-done.64
  914.1 2.3 bitcast_add_fusion
  917.4 2.1 bitcast_add_fusion.1
  919.6 2.0 collective-permute-start.59
  921.6 41.2 %collective-permute-done.65 = bf16[2,128,1024]{2,1,0:T(8,128)(2,1)S(1)} collective-permute-done((bf16[2,128,1024]{2,1,0:T(8,128)(2,1)S(1)}, bf16[2,128,1024]{2,1,0:T(8,128)(2,1)S(1)}, u32[]{:S(2)}, u32[]{:S(2)}) %collective-permute-start.65) | collective-permute-done | bytes 524320 | tf_op jit(solution)/shard_map/ppermute | solution.py:398
  963.0 1.8 collective-permute-start.66
  964.8 7.0 collective-permute-done.59
  972.1 1.6 maximum_select_fusion.2
  973.7 10.6 %collective-permute-done.66 = bf16[128,1024]{1,0:T(8,128)(2,1)S(1)} collective-permute-done((bf16[128,1024]{1,0:T(8,128)(2,1)S(1)}, bf16[128,1024]{1,0:T(8,128)(2,1)S(1)}, u32[]{:S(2)}, u32[]{:S(2)}) %collective-permute-start.66) | collective-permute-done | bytes 262176 | tf_op jit(solution)/shard_map/ppermute | solution.py:398
  985.4 3.4 collective-permute-done.60
  (275 shorter events, 67.2 us)
Async XLA Ops:
  8.2 31.1 %collective-permute-start.19 = (bf16[400,256]{1,0:T(8,128)(2,1)S(1)}, bf16[400,256]{1,0:T(8,128)(2,1)S(1)}, u32[]{:S(2)}, u32[]{:S(2)}) collective-permute-start(bf16[400,256]{1,0:T(8,128)(2,1)S(1)} %concatenate.57), channel_id=1, source_target_pairs={{0,2},{1,3},{2,0},{3,1},{4,6},{5,7},{6,4},{7,5},{8,10},{9,11},{10,... | collective-permute-start | bytes 614408 | tf_op jit(solution)/shard_map/ppermute | solution.py:398
  14.2 58.2 %collective-permute-start.10 = (bf16[1280,128]{1,0:T(8,128)(2,1)S(1)}, bf16[1280,128]{1,0:T(8,128)(2,1)S(1)}, u32[]{:S(2)}, u32[]{:S(2)}) collective-permute-start(bf16[1280,128]{1,0:T(8,128)(2,1)S(1)} %constant_dynamic-update-slice_fusion), channel_id=1, source_target_pairs={{0,2},{1,3},{2,0},{3,1},{4,6},{5,7},{6,4},{7,5},{8,10},{9,11},{10,... | collective-permute-start | bytes 983048 | tf_op jit(solution)/shard_map/ppermute | solution.py:398
  14.3 56.3 %collective-permute-start.1 = (bf16[128,1024]{1,0:T(8,128)(2,1)}, bf16[128,1024]{1,0:T(8,128)(2,1)}, u32[]{:S(2)}, u32[]{:S(2)}) collective-permute-start(bf16[128,1024]{1,0:T(8,128)(2,1)} %param.31), channel_id=1, source_target_pairs={{0,2},{1,3},{2,0},{3,1},{4,6},{5,7},{6,4},{7,5},{8,10},{9,11},{10,... | collective-permute-start | bytes 786440 | tf_op jit(solution)/shard_map/ppermute | solution.py:398
  20.3 107.5 %collective-permute-start.28 = (bf16[512,1024]{1,0:T(8,128)(2,1)}, bf16[512,1024]{1,0:T(8,128)(2,1)}, u32[]{:S(2)}, u32[]{:S(2)}) collective-permute-start(bf16[512,1024]{1,0:T(8,128)(2,1)} %get-tuple-element.185), channel_id=1, source_target_pairs={{0,0},{1,2},{2,4},{3,6},{4,1},{5,3},{6,5},{7,7},{8,8},{9,10},{10,1... | collective-permute-start | bytes 3145736 | tf_op jit(solution)/shard_map/ppermute | solution.py:415
  29.9 99.5 %collective-permute-start.29 = (bf16[512,1024]{1,0:T(8,128)(2,1)}, bf16[512,1024]{1,0:T(8,128)(2,1)}, u32[]{:S(2)}, u32[]{:S(2)}) collective-permute-start(bf16[512,1024]{1,0:T(8,128)(2,1)} %get-tuple-element.184), channel_id=1, source_target_pairs={{0,2},{1,0},{2,6},{3,4},{4,3},{5,1},{6,7},{7,5},{8,10},{9,8},{10,1... | collective-permute-start | bytes 3145736 | tf_op jit(solution)/shard_map/ppermute | solution.py:415
  39.4 36.0 %collective-permute-start = (s32[2,1,8]{2,1,0:T(1,128)S(1)}, s32[2,1,8]{2,1,0:T(1,128)S(1)}, u32[]{:S(2)}, u32[]{:S(2)}) collective-permute-start(s32[2,1,8]{2,1,0:T(1,128)S(1)} %copy-done.29), channel_id=1, source_target_pairs={{0,4},{1,5},{2,6},{3,7},{4,0},{5,1},{6,2},{7,3},{8,12},{9,13},{10,... | collective-permute-start | bytes 200 | tf_op jit(solution)/shard_map/ppermute | solution.py:398
  70.6 22.0 %collective-permute-start.20 = (bf16[2,400,256]{2,1,0:T(8,128)(2,1)}, bf16[2,400,256]{2,1,0:T(8,128)(2,1)}, u32[]{:S(2)}, u32[]{:S(2)}) collective-permute-start(bf16[2,400,256]{2,1,0:T(8,128)(2,1)} %pad_maximum_fusion.5), channel_id=1, source_target_pairs={{0,1},{1,0},{2,3},{3,2},{4,5},{5,4},{6,7},{7,6},{8,9},{9,8},{10,11... | collective-permute-start | bytes 1228808 | tf_op jit(solution)/shard_map/ppermute | solution.py:398
  72.4 39.0 %collective-permute-start.2 = (bf16[2,128,1024]{2,1,0:T(8,128)(2,1)}, bf16[2,128,1024]{2,1,0:T(8,128)(2,1)}, u32[]{:S(2)}, u32[]{:S(2)}) collective-permute-start(bf16[2,128,1024]{2,1,0:T(8,128)(2,1)} %pad_maximum_fusion.4), channel_id=1, source_target_pairs={{0,1},{1,0},{2,3},{3,2},{4,5},{5,4},{6,7},{7,6},{8,9},{9,8},{10,11... | collective-permute-start | bytes 1572872 | tf_op jit(solution)/shard_map/ppermute | solution.py:398
  75.3 52.4 %collective-permute-start.11 = (bf16[2,1280,128]{2,1,0:T(8,128)(2,1)}, bf16[2,1280,128]{2,1,0:T(8,128)(2,1)}, u32[]{:S(2)}, u32[]{:S(2)}) collective-permute-start(bf16[2,1280,128]{2,1,0:T(8,128)(2,1)} %pad_maximum_fusion.3), channel_id=1, source_target_pairs={{0,1},{1,0},{2,3},{3,2},{4,5},{5,4},{6,7},{7,6},{8,9},{9,8},{10,11... | collective-permute-start | bytes 1966088 | tf_op jit(solution)/shard_map/ppermute | solution.py:398
  92.5 39.8 %collective-permute-start.33 = (bf16[512,1024]{1,0:T(8,128)(2,1)}, bf16[512,1024]{1,0:T(8,128)(2,1)S(1)}, u32[]{:S(2)}, u32[]{:S(2)}) collective-permute-start(bf16[512,1024]{1,0:T(8,128)(2,1)} %get-tuple-element.182), channel_id=1, source_target_pairs={{0,0},{1,2},{2,4},{3,6},{4,1},{5,3},{6,5},{7,7},{8,8},{9,10},{10,1... | collective-permute-start | bytes 3145736 | tf_op jit(solution)/shard_map/ppermute | solution.py:415
  111.4 38.9 %collective-permute-start.34 = (bf16[512,1024]{1,0:T(8,128)(2,1)}, bf16[512,1024]{1,0:T(8,128)(2,1)}, u32[]{:S(2)}, u32[]{:S(2)}) collective-permute-start(bf16[512,1024]{1,0:T(8,128)(2,1)} %get-tuple-element.183), channel_id=1, source_target_pairs={{0,2},{1,0},{2,6},{3,4},{4,3},{5,1},{6,7},{7,5},{8,10},{9,8},{10,1... | collective-permute-start | bytes 3145736 | tf_op jit(solution)/shard_map/ppermute | solution.py:415
  127.8 24.4 %collective-permute-start.21 = (bf16[4,400,256]{2,1,0:T(8,128)(2,1)S(1)}, bf16[4,400,256]{2,1,0:T(8,128)(2,1)}, u32[]{:S(2)}, u32[]{:S(2)}) collective-permute-start(bf16[4,400,256]{2,1,0:T(8,128)(2,1)S(1)} %pad_maximum_fusion.2.refs_0_), channel_id=1, source_target_pairs={{0,4},{1,5},{2,6},{3,7},{4,0},{5,1},{6,2},{7,3},{8,12},{9,13},{10,... | collective-permute-start | bytes 2457608 | tf_op jit(solution)/shard_map/ppermute | solution.py:398
  127.8 24.4 %collective-permute-start.22 = (bf16[4,400,256]{2,1,0:T(8,128)(2,1)S(1)}, bf16[4,400,256]{2,1,0:T(8,128)(2,1)}, u32[]{:S(2)}, u32[]{:S(2)}) collective-permute-start(bf16[4,400,256]{2,1,0:T(8,128)(2,1)S(1)} %pad_maximum_fusion.2.refs_0_), channel_id=1, source_target_pairs={{0,8},{1,9},{2,10},{3,11},{4,12},{5,13},{6,14},{7,15},{8,0},{9,1},... | collective-permute-start | bytes 2457608 | tf_op jit(solution)/shard_map/ppermute | solution.py:398
  129.3 23.4 %collective-permute-start.24 = (bf16[4,400,256]{2,1,0:T(8,128)(2,1)S(1)}, bf16[4,400,256]{2,1,0:T(8,128)(2,1)}, u32[]{:S(2)}, u32[]{:S(2)}) collective-permute-start(bf16[4,400,256]{2,1,0:T(8,128)(2,1)S(1)} %pad_maximum_fusion.2.refs_0_), channel_id=1, source_target_pairs={{0,16},{1,17},{2,18},{3,19},{4,20},{5,21},{6,22},{7,23},{8,24},{9,... | collective-permute-start | bytes 2457608 | tf_op jit(solution)/shard_map/ppermute | solution.py:398
  132.3 38.7 %collective-permute-start.4 = (bf16[4,128,1024]{2,1,0:T(8,128)(2,1)S(1)}, bf16[4,128,1024]{2,1,0:T(8,128)(2,1)}, u32[]{:S(2)}, u32[]{:S(2)}) collective-permute-start(bf16[4,128,1024]{2,1,0:T(8,128)(2,1)S(1)} %pad_maximum_fusion.1.refs_0_), channel_id=1, source_target_pairs={{0,8},{1,9},{2,10},{3,11},{4,12},{5,13},{6,14},{7,15},{8,0},{9,1},... | collective-permute-start | bytes 3145736 | tf_op jit(solution)/shard_map/ppermute | solution.py:398
  150.2 22.3 %collective-permute-start.6 = (bf16[4,128,1024]{2,1,0:T(8,128)(2,1)S(1)}, bf16[4,128,1024]{2,1,0:T(8,128)(2,1)}, u32[]{:S(2)}, u32[]{:S(2)}) collective-permute-start(bf16[4,128,1024]{2,1,0:T(8,128)(2,1)S(1)} %pad_maximum_fusion.1.refs_0_), channel_id=1, source_target_pairs={{0,16},{1,17},{2,18},{3,19},{4,20},{5,21},{6,22},{7,23},{8,24},{9,... | collective-permute-start | bytes 3145736 | tf_op jit(solution)/shard_map/ppermute | solution.py:398
  152.1 22.4 %collective-permute-start.3 = (bf16[4,128,1024]{2,1,0:T(8,128)(2,1)S(1)}, bf16[4,128,1024]{2,1,0:T(8,128)(2,1)}, u32[]{:S(2)}, u32[]{:S(2)}) collective-permute-start(bf16[4,128,1024]{2,1,0:T(8,128)(2,1)S(1)} %pad_maximum_fusion.1.refs_0_), channel_id=1, source_target_pairs={{0,4},{1,5},{2,6},{3,7},{4,0},{5,1},{6,2},{7,3},{8,12},{9,13},{10,... | collective-permute-start | bytes 3145736 | tf_op jit(solution)/shard_map/ppermute | solution.py:398
  152.2 23.1 %collective-permute-start.30 = (bf16[512,1024]{1,0:T(8,128)(2,1)}, bf16[512,1024]{1,0:T(8,128)(2,1)}, u32[]{:S(2)}, u32[]{:S(2)}) collective-permute-start(bf16[512,1024]{1,0:T(8,128)(2,1)} %collective-permute-done.28.refs_8_), channel_id=1, source_target_pairs={{0,4},{1,5},{2,6},{3,7},{4,0},{5,1},{6,2},{7,3},{8,12},{9,13},{10,... | collective-permute-start | bytes 3145736 | tf_op jit(solution)/shard_map/ppermute | solution.py:398
  152.7 22.7 %collective-permute-start.31 = (bf16[512,1024]{1,0:T(8,128)(2,1)}, bf16[512,1024]{1,0:T(8,128)(2,1)}, u32[]{:S(2)}, u32[]{:S(2)}) collective-permute-start(bf16[512,1024]{1,0:T(8,128)(2,1)} %collective-permute-done.29.refs_9_), channel_id=1, source_target_pairs={{0,4},{1,5},{2,6},{3,7},{4,0},{5,1},{6,2},{7,3},{8,12},{9,13},{10,... | collective-permute-start | bytes 3145736 | tf_op jit(solution)/shard_map/ppermute | solution.py:398
  171.0 49.3 %collective-permute-start.15 = (bf16[4,1280,128]{2,1,0:T(8,128)(2,1)S(1)}, bf16[4,1280,128]{2,1,0:T(8,128)(2,1)}, u32[]{:S(2)}, u32[]{:S(2)}) collective-permute-start(bf16[4,1280,128]{2,1,0:T(8,128)(2,1)S(1)} %pad_maximum_fusion.refs_8_), channel_id=1, source_target_pairs={{0,16},{1,17},{2,18},{3,19},{4,20},{5,21},{6,22},{7,23},{8,24},{9,... | collective-permute-start | bytes 3932168 | tf_op jit(solution)/shard_map/ppermute | solution.py:398
  172.6 46.4 %collective-permute-start.26 = (bf16[4,400,256]{2,1,0:T(8,128)(2,1)}, bf16[4,400,256]{2,1,0:T(8,128)(2,1)}, u32[]{:S(2)}, u32[]{:S(2)}) collective-permute-start(bf16[4,400,256]{2,1,0:T(8,128)(2,1)} %collective-permute-done.22.refs_2_), channel_id=1, source_target_pairs={{0,16},{1,17},{2,18},{3,19},{4,20},{5,21},{6,22},{7,23},{8,24},{9,... | collective-permute-start | bytes 2457608 | tf_op jit(solution)/shard_map/ppermute | solution.py:398
  174.5 50.4 %collective-permute-start.13 = (bf16[4,1280,128]{2,1,0:T(8,128)(2,1)S(1)}, bf16[4,1280,128]{2,1,0:T(8,128)(2,1)}, u32[]{:S(2)}, u32[]{:S(2)}) collective-permute-start(bf16[4,1280,128]{2,1,0:T(8,128)(2,1)S(1)} %pad_maximum_fusion.refs_8_), channel_id=1, source_target_pairs={{0,8},{1,9},{2,10},{3,11},{4,12},{5,13},{6,14},{7,15},{8,0},{9,1},... | collective-permute-start | bytes 3932168 | tf_op jit(solution)/shard_map/ppermute | solution.py:398
  175.3 44.5 %collective-permute-start.23 = (bf16[4,400,256]{2,1,0:T(8,128)(2,1)}, bf16[4,400,256]{2,1,0:T(8,128)(2,1)}, u32[]{:S(2)}, u32[]{:S(2)}) collective-permute-start(bf16[4,400,256]{2,1,0:T(8,128)(2,1)} %collective-permute-done.22.refs_2_), channel_id=1, source_target_pairs={{0,4},{1,5},{2,6},{3,7},{4,0},{5,1},{6,2},{7,3},{8,12},{9,13},{10,... | collective-permute-start | bytes 2457608 | tf_op jit(solution)/shard_map/ppermute | solution.py:398
  175.5 47.1 %collective-permute-start.25 = (bf16[4,400,256]{2,1,0:T(8,128)(2,1)}, bf16[4,400,256]{2,1,0:T(8,128)(2,1)}, u32[]{:S(2)}, u32[]{:S(2)}) collective-permute-start(bf16[4,400,256]{2,1,0:T(8,128)(2,1)} %collective-permute-done.24.refs_4_), channel_id=1, source_target_pairs={{0,4},{1,5},{2,6},{3,7},{4,0},{5,1},{6,2},{7,3},{8,12},{9,13},{10,... | collective-permute-start | bytes 2457608 | tf_op jit(solution)/shard_map/ppermute | solution.py:398
  220.3 31.1 %collective-permute-start.17 = (bf16[4,1280,128]{2,1,0:T(8,128)(2,1)}, bf16[4,1280,128]{2,1,0:T(8,128)(2,1)}, u32[]{:S(2)}, u32[]{:S(2)}) collective-permute-start(bf16[4,1280,128]{2,1,0:T(8,128)(2,1)} %collective-permute-done.15.refs_12_), channel_id=1, source_target_pairs={{0,8},{1,9},{2,10},{3,11},{4,12},{5,13},{6,14},{7,15},{8,0},{9,1},... | collective-permute-start | bytes 3932168 | tf_op jit(solution)/shard_map/ppermute | solution.py:398
  222.6 25.2 %collective-permute-start.8 = (bf16[4,128,1024]{2,1,0:T(8,128)(2,1)}, bf16[4,128,1024]{2,1,0:T(8,128)(2,1)}, u32[]{:S(2)}, u32[]{:S(2)}) collective-permute-start(bf16[4,128,1024]{2,1,0:T(8,128)(2,1)} %collective-permute-done.4.refs_2_), channel_id=1, source_target_pairs={{0,16},{1,17},{2,18},{3,19},{4,20},{5,21},{6,22},{7,23},{8,24},{9,... | collective-permute-start | bytes 3145736 | tf_op jit(solution)/shard_map/ppermute | solution.py:398
  224.9 119.6 %collective-permute-start.5 = (bf16[4,128,1024]{2,1,0:T(8,128)(2,1)}, bf16[4,128,1024]{2,1,0:T(8,128)(2,1)S(1)}, u32[]{:S(2)}, u32[]{:S(2)}) collective-permute-start(bf16[4,128,1024]{2,1,0:T(8,128)(2,1)} %collective-permute-done.4.refs_2_), channel_id=1, source_target_pairs={{0,4},{1,5},{2,6},{3,7},{4,0},{5,1},{6,2},{7,3},{8,12},{9,13},{10,... | collective-permute-start | bytes 3145736 | tf_op jit(solution)/shard_map/ppermute | solution.py:398
  225.0 131.7 %collective-permute-start.7 = (bf16[4,128,1024]{2,1,0:T(8,128)(2,1)}, bf16[4,128,1024]{2,1,0:T(8,128)(2,1)}, u32[]{:S(2)}, u32[]{:S(2)}) collective-permute-start(bf16[4,128,1024]{2,1,0:T(8,128)(2,1)} %collective-permute-done.6.refs_4_), channel_id=1, source_target_pairs={{0,4},{1,5},{2,6},{3,7},{4,0},{5,1},{6,2},{7,3},{8,12},{9,13},{10,... | collective-permute-start | bytes 3145736 | tf_op jit(solution)/shard_map/ppermute | solution.py:398
  228.4 213.3 %collective-permute-start.16 = (bf16[4,1280,128]{2,1,0:T(8,128)(2,1)}, bf16[4,1280,128]{2,1,0:T(8,128)(2,1)}, u32[]{:S(2)}, u32[]{:S(2)}) collective-permute-start(bf16[4,1280,128]{2,1,0:T(8,128)(2,1)} %collective-permute-done.15.refs_12_), channel_id=1, source_target_pairs={{0,4},{1,5},{2,6},{3,7},{4,0},{5,1},{6,2},{7,3},{8,12},{9,13},{10,... | collective-permute-start | bytes 3932168 | tf_op jit(solution)/shard_map/ppermute | solution.py:398
  247.8 193.8 %collective-permute-start.14 = (bf16[4,1280,128]{2,1,0:T(8,128)(2,1)}, bf16[4,1280,128]{2,1,0:T(8,128)(2,1)}, u32[]{:S(2)}, u32[]{:S(2)}) collective-permute-start(bf16[4,1280,128]{2,1,0:T(8,128)(2,1)} %collective-permute-done.13.refs_10_), channel_id=1, source_target_pairs={{0,4},{1,5},{2,6},{3,7},{4,0},{5,1},{6,2},{7,3},{8,12},{9,13},{10,... | collective-permute-start | bytes 3932168 | tf_op jit(solution)/shard_map/ppermute | solution.py:398
  251.4 190.3 %collective-permute-start.18 = (bf16[4,1280,128]{2,1,0:T(8,128)(2,1)}, bf16[4,1280,128]{2,1,0:T(8,128)(2,1)}, u32[]{:S(2)}, u32[]{:S(2)}) collective-permute-start(bf16[4,1280,128]{2,1,0:T(8,128)(2,1)} %collective-permute-done.17.refs_14_), channel_id=1, source_target_pairs={{0,4},{1,5},{2,6},{3,7},{4,0},{5,1},{6,2},{7,3},{8,12},{9,13},{10,... | collective-permute-start | bytes 3932168 | tf_op jit(solution)/shard_map/ppermute | solution.py:398
  344.6 97.1 %collective-permute-start.9 = (bf16[4,128,1024]{2,1,0:T(8,128)(2,1)}, bf16[4,128,1024]{2,1,0:T(8,128)(2,1)S(1)}, u32[]{:S(2)}, u32[]{:S(2)}) collective-permute-start(bf16[4,128,1024]{2,1,0:T(8,128)(2,1)} %collective-permute-done.8.refs_6_), channel_id=1, source_target_pairs={{0,4},{1,5},{2,6},{3,7},{4,0},{5,1},{6,2},{7,3},{8,12},{9,13},{10,... | collective-permute-start | bytes 3145736 | tf_op jit(solution)/shard_map/ppermute | solution.py:398
  356.7 85.0 %collective-permute-start.32 = (bf16[1024,512]{1,0:T(8,128)(2,1)}, bf16[1024,512]{1,0:T(8,128)(2,1)S(1)}, u32[]{:S(2)}, u32[]{:S(2)}) collective-permute-start(bf16[1024,512]{1,0:T(8,128)(2,1)} %get-tuple-element.63.context_other), channel_id=1, source_target_pairs={{0,4},{1,5},{2,6},{3,7},{4,0},{5,1},{6,2},{7,3},{8,12},{9,13},{10,... | collective-permute-start | bytes 3145736 | tf_op jit(solution)/shard_map/ppermute | solution.py:398
  504.1 33.6 %collective-permute-start.37 = (bf16[1024,512]{1,0:T(8,128)(2,1)}, bf16[1024,512]{1,0:T(8,128)(2,1)}, u32[]{:S(2)}, u32[]{:S(2)}) collective-permute-start(bf16[1024,512]{1,0:T(8,128)(2,1)} %get-tuple-element.67), channel_id=1, source_target_pairs={{0,4},{1,5},{2,6},{3,7},{4,0},{5,1},{6,2},{7,3},{8,12},{9,13},{10,... | collective-permute-start | bytes 3145736 | tf_op jit(solution)/shard_map/ppermute | solution.py:398
  510.5 12.6 %collective-permute-start.49 = (bf16[2,4,128,256]{3,2,1,0:T(8,128)(2,1)}, bf16[2,4,128,256]{3,2,1,0:T(8,128)(2,1)S(1)}, u32[]{:S(2)}, u32[]{:S(2)}) collective-permute-start(bf16[2,4,128,256]{3,2,1,0:T(8,128)(2,1)} %get-tuple-element.82), channel_id=1, source_target_pairs={{0,4},{1,5},{2,6},{3,7},{4,0},{5,1},{6,2},{7,3},{8,12},{9,13},{10,... | collective-permute-start | bytes 1572872 | tf_op jit(solution)/shard_map/ppermute | solution.py:398
  522.7 264.5 %collective-permute-start.61 = (bf16[2,4,128,1024]{3,2,1,0:T(8,128)(2,1)}, bf16[2,4,128,1024]{3,2,1,0:T(8,128)(2,1)S(1)}, u32[]{:S(2)}, u32[]{:S(2)}) collective-permute-start(bf16[2,4,128,1024]{3,2,1,0:T(8,128)(2,1)} %get-tuple-element.96), channel_id=1, source_target_pairs={{0,4},{1,5},{2,6},{3,7},{4,0},{5,1},{6,2},{7,3},{8,12},{9,13},{10,... | collective-permute-start | bytes 6291464 | tf_op jit(solution)/shard_map/ppermute | solution.py:398
  530.9 175.2 %collective-permute-start.51 = (bf16[2,4,128,256]{3,2,1,0:T(8,128)(2,1)}, bf16[2,4,128,256]{3,2,1,0:T(8,128)(2,1)}, u32[]{:S(2)}, u32[]{:S(2)}) collective-permute-start(bf16[2,4,128,256]{3,2,1,0:T(8,128)(2,1)} %get-tuple-element.85), channel_id=1, source_target_pairs={{0,16},{1,17},{2,18},{3,19},{4,20},{5,21},{6,22},{7,23},{8,24},{9,... | collective-permute-start | bytes 1572872 | tf_op jit(solution)/shard_map/ppermute | solution.py:398
  534.0 201.6 %collective-permute-start.35 = (bf16[512,1024]{1,0:T(8,128)(2,1)}, bf16[512,1024]{1,0:T(8,128)(2,1)S(1)}, u32[]{:S(2)}, u32[]{:S(2)}) collective-permute-start(bf16[512,1024]{1,0:T(8,128)(2,1)} %get-tuple-element.180), channel_id=1, source_target_pairs={{0,0},{2,1},{4,2},{6,3},{1,4},{3,5},{5,6},{7,7},{8,8},{10,9},{12,1... | collective-permute-start | bytes 3145736 | tf_op jit(solution)/shard_map/ppermute | solution.py:423
  535.9 199.8 %collective-permute-start.36 = (bf16[512,1024]{1,0:T(8,128)(2,1)}, bf16[512,1024]{1,0:T(8,128)(2,1)}, u32[]{:S(2)}, u32[]{:S(2)}) collective-permute-start(bf16[512,1024]{1,0:T(8,128)(2,1)} %get-tuple-element.181), channel_id=1, source_target_pairs={{2,0},{0,1},{6,2},{4,3},{3,4},{1,5},{7,6},{5,7},{10,8},{8,9},{14,1... | collective-permute-start | bytes 3145736 | tf_op jit(solution)/shard_map/ppermute | solution.py:424
  703.4 32.8 %collective-permute-start.41 = (bf16[2,2,3,128,256]{4,3,2,1,0:T(8,128)(2,1)}, bf16[2,2,3,128,256]{4,3,2,1,0:T(8,128)(2,1)}, u32[]{:S(2)}, u32[]{:S(2)}) collective-permute-start(bf16[2,2,3,128,256]{4,3,2,1,0:T(8,128)(2,1)} %get-tuple-element.76), channel_id=1, source_target_pairs={{0,8},{1,9},{2,10},{3,11},{4,12},{5,13},{6,14},{7,15},{8,0},{9,1},... | collective-permute-start | bytes 2359304 | tf_op jit(solution)/shard_map/ppermute | solution.py:398
  706.1 87.3 %collective-permute-start.62 = (bf16[2,4,128,1024]{3,2,1,0:T(8,128)(2,1)}, bf16[2,4,128,1024]{3,2,1,0:T(8,128)(2,1)}, u32[]{:S(2)}, u32[]{:S(2)}) collective-permute-start(bf16[2,4,128,1024]{3,2,1,0:T(8,128)(2,1)} %get-tuple-element.97), channel_id=1, source_target_pairs={{0,4},{1,5},{2,6},{3,7},{4,0},{5,1},{6,2},{7,3},{8,12},{9,13},{10,... | collective-permute-start | bytes 6291464 | tf_op jit(solution)/shard_map/ppermute | solution.py:398
  735.6 81.5 %collective-permute-start.55 = (bf16[2,4,128,1024]{3,2,1,0:T(8,128)(2,1)}, bf16[2,4,128,1024]{3,2,1,0:T(8,128)(2,1)}, u32[]{:S(2)}, u32[]{:S(2)}) collective-permute-start(bf16[2,4,128,1024]{3,2,1,0:T(8,128)(2,1)} %get-tuple-element.90), channel_id=1, source_target_pairs={{0,4},{1,5},{2,6},{3,7},{4,0},{5,1},{6,2},{7,3},{8,12},{9,13},{10,... | collective-permute-start | bytes 6291464 | tf_op jit(solution)/shard_map/ppermute | solution.py:398
  735.7 81.5 %collective-permute-start.56 = (bf16[2,4,128,1024]{3,2,1,0:T(8,128)(2,1)}, bf16[2,4,128,1024]{3,2,1,0:T(8,128)(2,1)}, u32[]{:S(2)}, u32[]{:S(2)}) collective-permute-start(bf16[2,4,128,1024]{3,2,1,0:T(8,128)(2,1)} %get-tuple-element.91), channel_id=1, source_target_pairs={{0,4},{1,5},{2,6},{3,7},{4,0},{5,1},{6,2},{7,3},{8,12},{9,13},{10,... | collective-permute-start | bytes 6291464 | tf_op jit(solution)/shard_map/ppermute | solution.py:398
  736.2 50.9 %collective-permute-start.44 = (bf16[2,2,3,128,256]{4,3,2,1,0:T(8,128)(2,1)}, bf16[2,2,3,128,256]{4,3,2,1,0:T(8,128)(2,1)}, u32[]{:S(2)}, u32[]{:S(2)}) collective-permute-start(bf16[2,2,3,128,256]{4,3,2,1,0:T(8,128)(2,1)} %get-tuple-element.78), channel_id=1, source_target_pairs={{0,4},{1,5},{2,6},{3,7},{4,0},{5,1},{6,2},{7,3},{8,12},{9,13},{10,... | collective-permute-start | bytes 2359304 | tf_op jit(solution)/shard_map/ppermute | solution.py:398
  787.1 20.4 %collective-permute-start.43 = (bf16[2,2,3,128,256]{4,3,2,1,0:T(8,128)(2,1)}, bf16[2,2,3,128,256]{4,3,2,1,0:T(8,128)(2,1)}, u32[]{:S(2)}, u32[]{:S(2)}) collective-permute-start(bf16[2,2,3,128,256]{4,3,2,1,0:T(8,128)(2,1)} %get-tuple-element.77), channel_id=1, source_target_pairs={{0,4},{1,5},{2,6},{3,7},{4,0},{5,1},{6,2},{7,3},{8,12},{9,13},{10,... | collective-permute-start | bytes 2359304 | tf_op jit(solution)/shard_map/ppermute | solution.py:398
  787.2 21.8 %collective-permute-start.45 = (bf16[2,2,3,128,256]{4,3,2,1,0:T(8,128)(2,1)}, bf16[2,2,3,128,256]{4,3,2,1,0:T(8,128)(2,1)}, u32[]{:S(2)}, u32[]{:S(2)}) collective-permute-start(bf16[2,2,3,128,256]{4,3,2,1,0:T(8,128)(2,1)} %collective-permute-done.44), channel_id=1, source_target_pairs={{0,8},{1,9},{2,10},{3,11},{4,12},{5,13},{6,14},{7,15},{8,0},{9,1},... | collective-permute-start | bytes 2359304 | tf_op jit(solution)/shard_map/ppermute | solution.py:398
  793.4 20.1 %collective-permute-start.52 = (bf16[4,128,256]{2,1,0:T(8,128)(2,1)S(1)}, bf16[4,128,256]{2,1,0:T(8,128)(2,1)S(1)}, u32[]{:S(2)}, u32[]{:S(2)}) collective-permute-start(bf16[4,128,256]{2,1,0:T(8,128)(2,1)S(1)} %fusion.8), channel_id=1, source_target_pairs={{0,8},{1,9},{2,10},{3,11},{4,12},{5,13},{6,14},{7,15},{8,0},{9,1},... | collective-permute-start | bytes 786440 | tf_op jit(solution)/shard_map/ppermute | solution.py:398
  807.6 24.1 %collective-permute-start.42 = (bf16[2,3,128,256]{3,2,1,0:T(8,128)(2,1)S(1)}, bf16[2,3,128,256]{3,2,1,0:T(8,128)(2,1)S(1)}, u32[]{:S(2)}, u32[]{:S(2)}) collective-permute-start(bf16[2,3,128,256]{3,2,1,0:T(8,128)(2,1)S(1)} %fusion.5), channel_id=1, source_target_pairs={{0,16},{1,17},{2,18},{3,19},{4,20},{5,21},{6,22},{7,23},{8,24},{9,... | collective-permute-start | bytes 1179656 | tf_op jit(solution)/shard_map/ppermute | solution.py:398
  809.1 78.0 %collective-permute-start.63 = (bf16[2,4,128,1024]{3,2,1,0:T(8,128)(2,1)}, bf16[2,4,128,1024]{3,2,1,0:T(8,128)(2,1)}, u32[]{:S(2)}, u32[]{:S(2)}) collective-permute-start(bf16[2,4,128,1024]{3,2,1,0:T(8,128)(2,1)} %get-tuple-element.99), channel_id=1, source_target_pairs={{0,16},{1,17},{2,18},{3,19},{4,20},{5,21},{6,22},{7,23},{8,24},{9,... | collective-permute-start | bytes 6291464 | tf_op jit(solution)/shard_map/ppermute | solution.py:398
  813.5 58.8 %collective-permute-start.46 = (bf16[2,3,128,256]{3,2,1,0:T(8,128)(2,1)S(1)}, bf16[2,3,128,256]{3,2,1,0:T(8,128)(2,1)S(1)}, u32[]{:S(2)}, u32[]{:S(2)}) collective-permute-start(bf16[2,3,128,256]{3,2,1,0:T(8,128)(2,1)S(1)} %fusion.6), channel_id=1, source_target_pairs={{0,16},{1,17},{2,18},{3,19},{4,20},{5,21},{6,22},{7,23},{8,24},{9,... | collective-permute-start | bytes 1179656 | tf_op jit(solution)/shard_map/ppermute | solution.py:398
  817.1 79.5 %collective-permute-start.38 = (bf16[1024,1024]{1,0:T(8,128)(2,1)}, bf16[1024,1024]{1,0:T(8,128)(2,1)}, u32[]{:S(2)}, u32[]{:S(2)}) collective-permute-start(bf16[1024,1024]{1,0:T(8,128)(2,1)} %token_grad.2), channel_id=1, source_target_pairs={{0,4},{1,5},{2,6},{3,7},{4,0},{5,1},{6,2},{7,3},{8,12},{9,13},{10,... | collective-permute-start | bytes 6291464 | tf_op jit(solution)/shard_map/ppermute | solution.py:398
  817.2 59.6 %collective-permute-start.53 = (bf16[2,128,256]{2,1,0:T(8,128)(2,1)S(1)}, bf16[2,128,256]{2,1,0:T(8,128)(2,1)S(1)}, u32[]{:S(2)}, u32[]{:S(2)}) collective-permute-start(bf16[2,128,256]{2,1,0:T(8,128)(2,1)S(1)} %slice.424), channel_id=1, source_target_pairs={{0,1},{1,0},{2,3},{3,2},{4,5},{5,4},{6,7},{7,6},{8,9},{9,8},{10,11... | collective-permute-start | bytes 393224 | tf_op jit(solution)/shard_map/ppermute | solution.py:398
  831.7 60.2 %collective-permute-start.57 = (bf16[2,4,128,1024]{3,2,1,0:T(8,128)(2,1)}, bf16[2,4,128,1024]{3,2,1,0:T(8,128)(2,1)}, u32[]{:S(2)}, u32[]{:S(2)}) collective-permute-start(bf16[2,4,128,1024]{3,2,1,0:T(8,128)(2,1)} %get-tuple-element.93), channel_id=1, source_target_pairs={{0,8},{1,9},{2,10},{3,11},{4,12},{5,13},{6,14},{7,15},{8,0},{9,1},... | collective-permute-start | bytes 6291464 | tf_op jit(solution)/shard_map/ppermute | solution.py:398
  874.6 12.3 %collective-permute-start.47 = (bf16[2,3,128,256]{3,2,1,0:T(8,128)(2,1)S(1)}, bf16[2,3,128,256]{3,2,1,0:T(8,128)(2,1)S(1)}, u32[]{:S(2)}, u32[]{:S(2)}) collective-permute-start(bf16[2,3,128,256]{3,2,1,0:T(8,128)(2,1)S(1)} %slice.423), channel_id=1, source_target_pairs={{0,1},{1,0},{2,3},{3,2},{4,5},{5,4},{6,7},{7,6},{8,9},{9,8},{10,11... | collective-permute-start | bytes 1179656 | tf_op jit(solution)/shard_map/ppermute | solution.py:398
  876.9 18.9 %collective-permute-start.54 = (bf16[128,256]{1,0:T(8,128)(2,1)S(1)}, bf16[128,256]{1,0:T(8,128)(2,1)S(1)}, u32[]{:S(2)}, u32[]{:S(2)}) collective-permute-start(bf16[128,256]{1,0:T(8,128)(2,1)S(1)} %fusion.16), channel_id=1, source_target_pairs={{0,2},{1,3},{2,0},{3,1},{4,6},{5,7},{6,4},{7,5},{8,10},{9,11},{10,... | collective-permute-start | bytes 196616 | tf_op jit(solution)/shard_map/ppermute | solution.py:398
  889.9 24.3 %collective-permute-start.64 = (bf16[4,128,1024]{2,1,0:T(8,128)(2,1)}, bf16[4,128,1024]{2,1,0:T(8,128)(2,1)}, u32[]{:S(2)}, u32[]{:S(2)}) collective-permute-start(bf16[4,128,1024]{2,1,0:T(8,128)(2,1)} %fusion.1), channel_id=1, source_target_pairs={{0,8},{1,9},{2,10},{3,11},{4,12},{5,13},{6,14},{7,15},{8,0},{9,1},... | collective-permute-start | bytes 3145736 | tf_op jit(solution)/shard_map/ppermute | solution.py:398
  890.6 20.2 %collective-permute-start.48 = (bf16[3,128,256]{2,1,0:T(8,128)(2,1)S(1)}, bf16[3,128,256]{2,1,0:T(8,128)(2,1)S(1)}, u32[]{:S(2)}, u32[]{:S(2)}) collective-permute-start(bf16[3,128,256]{2,1,0:T(8,128)(2,1)S(1)} %fusion.11), channel_id=1, source_target_pairs={{0,2},{1,3},{2,0},{3,1},{4,6},{5,7},{6,4},{7,5},{8,10},{9,11},{10,... | collective-permute-start | bytes 589832 | tf_op jit(solution)/shard_map/ppermute | solution.py:398
  894.5 22.9 %collective-permute-start.58 = (bf16[4,128,1024]{2,1,0:T(8,128)(2,1)}, bf16[4,128,1024]{2,1,0:T(8,128)(2,1)}, u32[]{:S(2)}, u32[]{:S(2)}) collective-permute-start(bf16[4,128,1024]{2,1,0:T(8,128)(2,1)} %fusion), channel_id=1, source_target_pairs={{0,16},{1,17},{2,18},{3,19},{4,20},{5,21},{6,22},{7,23},{8,24},{9,... | collective-permute-start | bytes 3145736 | tf_op jit(solution)/shard_map/ppermute | solution.py:398
  907.8 64.3 %collective-permute-start.39 = (bf16[512,1024]{1,0:T(8,128)(2,1)S(1)}, bf16[512,1024]{1,0:T(8,128)(2,1)S(1)}, u32[]{:S(2)}, u32[]{:S(2)}) collective-permute-start(bf16[512,1024]{1,0:T(8,128)(2,1)S(1)} %get-tuple-element.178), channel_id=1, source_target_pairs={{0,0},{2,1},{4,2},{6,3},{1,4},{3,5},{5,6},{7,7},{8,8},{10,9},{12,1... | collective-permute-start | bytes 3145736 | tf_op jit(solution)/shard_map/ppermute | solution.py:423
  908.5 63.6 %collective-permute-start.40 = (bf16[512,1024]{1,0:T(8,128)(2,1)S(1)}, bf16[512,1024]{1,0:T(8,128)(2,1)S(1)}, u32[]{:S(2)}, u32[]{:S(2)}) collective-permute-start(bf16[512,1024]{1,0:T(8,128)(2,1)S(1)} %get-tuple-element.179), channel_id=1, source_target_pairs={{2,0},{0,1},{6,2},{4,3},{3,4},{1,5},{7,6},{5,7},{10,8},{8,9},{14,1... | collective-permute-start | bytes 3145736 | tf_op jit(solution)/shard_map/ppermute | solution.py:424
  916.5 46.3 %collective-permute-start.65 = (bf16[2,128,1024]{2,1,0:T(8,128)(2,1)S(1)}, bf16[2,128,1024]{2,1,0:T(8,128)(2,1)S(1)}, u32[]{:S(2)}, u32[]{:S(2)}) collective-permute-start(bf16[2,128,1024]{2,1,0:T(8,128)(2,1)S(1)} %slice.421), channel_id=1, source_target_pairs={{0,1},{1,0},{2,3},{3,2},{4,5},{5,4},{6,7},{7,6},{8,9},{9,8},{10,11... | collective-permute-start | bytes 1572872 | tf_op jit(solution)/shard_map/ppermute | solution.py:398
  919.6 52.2 %collective-permute-start.59 = (bf16[2,128,1024]{2,1,0:T(8,128)(2,1)S(1)}, bf16[2,128,1024]{2,1,0:T(8,128)(2,1)S(1)}, u32[]{:S(2)}, u32[]{:S(2)}) collective-permute-start(bf16[2,128,1024]{2,1,0:T(8,128)(2,1)S(1)} %slice.422), channel_id=1, source_target_pairs={{0,1},{1,0},{2,3},{3,2},{4,5},{5,4},{6,7},{7,6},{8,9},{9,8},{10,11... | collective-permute-start | bytes 1572872 | tf_op jit(solution)/shard_map/ppermute | solution.py:398
  963.0 21.4 %collective-permute-start.66 = (bf16[128,1024]{1,0:T(8,128)(2,1)S(1)}, bf16[128,1024]{1,0:T(8,128)(2,1)S(1)}, u32[]{:S(2)}, u32[]{:S(2)}) collective-permute-start(bf16[128,1024]{1,0:T(8,128)(2,1)S(1)} %fusion.10), channel_id=1, source_target_pairs={{0,2},{1,3},{2,0},{3,1},{4,6},{5,7},{6,4},{7,5},{8,10},{9,11},{10,... | collective-permute-start | bytes 786440 | tf_op jit(solution)/shard_map/ppermute | solution.py:398
  972.0 16.8 %collective-permute-start.60 = (bf16[128,1024]{1,0:T(8,128)(2,1)S(1)}, bf16[128,1024]{1,0:T(8,128)(2,1)S(1)}, u32[]{:S(2)}, u32[]{:S(2)}) collective-permute-start(bf16[128,1024]{1,0:T(8,128)(2,1)S(1)} %fusion.9), channel_id=1, source_target_pairs={{0,2},{1,3},{2,0},{3,1},{4,6},{5,7},{6,4},{7,5},{8,10},{9,11},{10,... | collective-permute-start | bytes 786440 | tf_op jit(solution)/shard_map/ppermute | solution.py:398
  (33 other events, 965.5 us)
